TPU v7x, 128 devices: a whole 4x4x4 slice. The times are simulated.
128 devices in a mesh: row: 4 (over x), col: 32 (over z, y, core).
Axes of the slice: x: 4, y: 4, z: 4, core: 2. Of those that a mesh axis runs over, the one named last changes fastest.
Arguments:
- cells: float32 [128, 128, 128], P(('row', 'col')), may hold values from 0 to 1
- target: float32 [1024, 12288], P('row', 'col'), may hold values from 0 to 1
- row_taps: bfloat16 [24, 2, 35], replicated, may hold values from -1 to 1
- col_taps: bfloat16 [24, 2, 35], replicated, may hold values from -1 to 1
- socs: float32 [12], replicated, may hold values from 0.05 to 1
- cell_of_block: int32 [8, 96], P('row', 'col'), may hold values from 0 to 127
- owner_map: int32 [128], replicated, may hold values from 0 to 127, each once
Outputs:
- cell_gradient: float32 [128, 128, 128], P(('row', 'col'))
- new_mask: float32 [1024, 12288], P('row', 'col')
Inputs may be any that keep to these rules, and one draw needn't show every extreme that they name: `owner_map`: every store position appears exactly once.
All inputs are finite; a program needn't handle non-finite values.
Results may differ from a plain program's by a relative error of at most 0.0063.
Values may be sent and summed in bfloat16 or wider, within the bound.
No kernel may reach another device: no remote copies, remote signals or barrier semaphores. Data moves between devices by JAX's collectives and lax.ppermute only.
A program may use at most 64 MiB of HBM per device.

v0:
```python
import jax
import jax.numpy as jnp
from jax import lax
from jax.sharding import PartitionSpec as P


def with_halo(block, sides, width):
    for axis, dim in sides:
        count = lax.axis_size(axis)
        forward = [(i, i + 1) for i in range(count - 1)]
        backward = [(target, source) for source, target in forward]
        low = lax.ppermute(
            lax.slice_in_dim(block, block.shape[dim] - width, None, axis=dim), axis, forward
        )
        high = lax.ppermute(lax.slice_in_dim(block, 0, width, axis=dim), axis, backward)
        block = jnp.concatenate([low, block, high], axis=dim)
    return block


def banded(taps, size):
    count = taps.shape[1]
    padded_taps = jnp.concatenate([taps, jnp.zeros((taps.shape[0], size), taps.dtype)], 1)
    flat = jnp.tile(padded_taps, (1, size))[:, : size * (size + count - 1)]
    return flat.reshape(taps.shape[0], size, size + count - 1)


def separable(padded, row_part, col_part):
    count = row_part.shape[1]
    out_cols = padded.shape[1] - count + 1
    col_size = min(128, out_cols)
    col_blocks = -(-out_cols // col_size)
    wide_cols = jnp.pad(padded, ((0, 0), (0, col_blocks * col_size - out_cols)))
    col_matrix = banded(col_part, col_size)
    pieces = []
    for index in range(col_blocks):
        window = wide_cols[:, index * col_size : index * col_size + col_size + count - 1]
        pieces.append(
            jnp.einsum("ab,rcb->rac", window, col_matrix, preferred_element_type=jnp.float32)
        )
    columns = jnp.concatenate(pieces, 2)[:, :, :out_cols].astype(jnp.bfloat16)
    out_rows = columns.shape[1] - count + 1
    row_size = min(128, out_rows)
    row_blocks = -(-out_rows // row_size)
    wide_rows = jnp.pad(columns, ((0, 0), (0, row_blocks * row_size - out_rows), (0, 0)))
    row_matrix = banded(row_part, row_size)
    parts = []
    for index in range(row_blocks):
        window = wide_rows[:, index * row_size : index * row_size + row_size + count - 1, :]
        parts.append(
            jnp.einsum("rda,rac->dc", row_matrix, window, preferred_element_type=jnp.float32)
        )
    return jnp.concatenate(parts, 0)[:out_rows]


def per_device(cells, target, row_taps, col_taps, socs, cell_of_block, owner_map):
    blk = cells.shape[1]
    tile_rows, tile_cols = target.shape
    half = row_taps.shape[2] // 2
    chan = row_taps.shape[0]
    cells_total = owner_map.shape[0]
    own_count = cells.shape[0]
    nblocks = cell_of_block.shape[0] * cell_of_block.shape[1]
    place_ids = cell_of_block.reshape(-1)
    table = place_ids[:, None] == jnp.arange(cells_total, dtype=jnp.int32)[None, :]
    positions = jnp.sum(jnp.where(table, owner_map[None, :], 0), axis=1)
    weights = socs / jnp.sum(socs)
    flat_cells = cells.reshape(own_count, blk * blk)

    def assemble(blocks):
        shaped = blocks.reshape(tile_rows // blk, tile_cols // blk, blk, blk)
        return shaped.transpose(0, 2, 1, 3).reshape(tile_rows, tile_cols)

    def pick(piece):
        index = jnp.arange(piece.shape[0], dtype=jnp.int32)
        select = (positions[:, None] == index[None, :]).astype(piece.dtype)
        return jnp.dot(
            select, piece, preferred_element_type=jnp.float32, precision=lax.Precision.HIGHEST
        )

    placed = pick(
        lax.all_gather(flat_cells.astype(jnp.bfloat16), ("row", "col"), axis=0, tiled=True)
    )
    mask = assemble(placed).astype(jnp.bfloat16)
    padded = with_halo(mask, (("row", 0), ("col", 1)), half)

    def light(k, total):
        field = separable(padded, row_taps[k], col_taps[k])
        return total + weights[k // 2] * field * field

    intensity = lax.fori_loop(0, chan, light, jnp.zeros((tile_rows, tile_cols), jnp.float32))
    resist = jax.nn.sigmoid(3.0 * (intensity - 1.3))
    error = 2.0 * (resist - target) * 3.0 * resist * (1.0 - resist)

    def adjoint(k, total):
        field = separable(padded, row_taps[k], col_taps[k])
        weighted = (2.0 * weights[k // 2] * field * error).astype(jnp.bfloat16)
        weighted_wide = with_halo(weighted, (("row", 0), ("col", 1)), half)
        return total + separable(weighted_wide, row_taps[k][:, ::-1], col_taps[k][:, ::-1])

    slab_gradient = lax.fori_loop(0, chan, adjoint, jnp.zeros((tile_rows, tile_cols), jnp.float32))
    shaped = slab_gradient.reshape(tile_rows // blk, blk, tile_cols // blk, blk)
    blocks = shaped.transpose(0, 2, 1, 3).reshape(nblocks, blk * blk)
    index = jnp.arange(lax.axis_size(("row", "col")) * own_count, dtype=jnp.int32)
    select = (index[:, None] == positions[None, :]).astype(jnp.float32)
    cell_gradient = lax.psum_scatter(
        jnp.dot(
            select, blocks, preferred_element_type=jnp.float32, precision=lax.Precision.HIGHEST
        ),
        ("row", "col"),
        scatter_dimension=0,
        tiled=True,
    )
    updated = flat_cells - 0.05 * cell_gradient
    new_blocks = pick(lax.all_gather(updated, ("row", "col"), axis=0, tiled=True))
    return (cell_gradient.reshape(own_count, blk, blk), assemble(new_blocks))


def solution(mesh):
    in_specs = (P(("row", "col"), None, None), P("row", "col"), P(), P(), P(), P("row", "col"), P())
    out_specs = (P(("row", "col"), None, None), P("row", "col"))
    return jax.shard_map(
        per_device, mesh=mesh, in_specs=in_specs, out_specs=out_specs, check_vma=False
    )
```

profile of v0, /device:TPU:1, one launch (start us, length us, event | category | flops | bytes accessed | tf_op | source)
XLA Modules:
  0.0 1084.8 jit_solution(12306343201773807410)
XLA Ops:
  10.4 74.4 %all-gather.5.cloned.1.call-done = bf16[128,1,16384]{2,1,0:T(2,128)(2,1)} async-done(((bf16[1,1,16384]{2,1,0:T(2,128)(2,1)}), bf16[128,1,16384]{2,1,0:T(2,128)(2,1)}) %all-gather.5.cloned.1.call-update) | async-done | bytes 4194320 | tf_op jit(solution)/shard_map/all_gather | solution.py:81
  84.8 7.8 fusion.46
  109.5 132.3 %while.32 = (s32[]{:T(128)}, f32[256,384]{1,0:T(8,128)S(1)}, f32[12]{0:T(128)S(1)}, bf16[24,2,35]{2,1,0:T(2,128)(2,1)}, bf16[24,2,35]{2,1,0:T(2,128)(2,1)}, /*in...) while((s32[]{:T(128)}, f32[256,384]{1,0:T(8,128)S(1)}, ...), condition=%wide.region_3.4_spmd.clone, body=%wide.region_2.3_spmd.clone.sunk | while | flops 137912832 | bytes 5635703 | solution.py:90
  242.0 575.4 %while.33 = (s32[]{:T(128)}, f32[256,384]{1,0:T(8,128)S(1)}, bf16[24,2,35]{2,1,0:T(2,128)(2,1)}, bf16[24,2,35]{2,1,0:T(2,128)(2,1)}, f32[12]{0:T(128)S(1)}, /*in...) while((s32[]{:T(128)}, f32[256,384]{1,0:T(8,128)S(1)}, ...), condition=%wide.region_5.6_spmd.clone, body=%wide.region_4.5_spmd.clone.sunk | while | flops 276950592 | bytes 11928551 | solution.py:100
  326.1 5.4 collective-permute-done.2
  350.2 5.6 collective-permute-done.2
  374.4 5.6 collective-permute-done.2
  398.6 5.6 collective-permute-done.2
  422.9 5.6 collective-permute-done.2
  447.1 5.6 collective-permute-done.2
  471.4 5.6 collective-permute-done.2
  495.6 5.6 collective-permute-done.2
  519.8 5.6 collective-permute-done.2
  544.1 5.6 collective-permute-done.2
  568.3 5.6 collective-permute-done.2
  592.5 5.6 collective-permute-done.2
  605.7 4.0 collective-permute-start.1
  616.8 5.6 collective-permute-done.2
  629.9 4.0 collective-permute-start.1
  641.0 5.6 collective-permute-done.2
  665.3 5.6 collective-permute-done.2
  689.5 5.6 collective-permute-done.2
  713.7 5.6 collective-permute-done.2
  738.0 5.6 collective-permute-done.2
  751.1 4.0 collective-permute-start.1
  762.2 5.6 collective-permute-done.2
  786.5 5.6 collective-permute-done.2
  810.7 5.6 collective-permute-done.2
  817.9 5.6 fusion.49
  823.8 170.4 %all-reduce.9.cloned.1.call-done = f32[128,16384]{1,0:T(8,128)} async-done(((f32[128,16384]{1,0:T(8,128)}), f32[128,16384]{1,0:T(8,128)}) %all-reduce.9.cloned.1.call-update) | async-done | bytes 8388624
  996.0 70.4 %all-gather.7.cloned.1.call-done = f32[128,1,16384]{2,1,0:T(1,128)} async-done(((f32[1,1,16384]{2,1,0:T(1,128)}), f32[128,1,16384]{2,1,0:T(1,128)}) %all-gather.7.cloned.1.call-update) | async-done | bytes 8388624 | tf_op jit(solution)/shard_map/all_gather | solution.py:114
  1066.5 10.5 fusion.43
  (1648 shorter events, 576.9 us)
Async XLA Ops:
  7.2 77.6 %all-gather.5.cloned.1.call-start = ((), (), s32[]{:S(2)}) async-start(), calls=%async_computation | async-start | bytes 8454144 | tf_op jit(solution)/shard_map/all_gather | solution.py:81
  8.8 985.5 %all-reduce.9.cloned.1.call-start = ((), (), s32[]{:S(2)}) async-start(), calls=%async_computation.2 | async-start | bytes 16777216
  323.9 7.6 collective-permute-start.2
  348.0 7.8 collective-permute-start.2
  372.2 7.8 collective-permute-start.2
  396.4 7.8 collective-permute-start.2
  420.7 7.8 collective-permute-start.2
  444.9 7.8 collective-permute-start.2
  469.1 7.8 collective-permute-start.2
  493.4 7.8 collective-permute-start.2
  517.6 7.8 collective-permute-start.2
  541.9 7.8 collective-permute-start.2
  555.9 7.3 collective-permute-start
  566.1 7.8 collective-permute-start.2
  580.2 7.3 collective-permute-start
  590.3 7.8 collective-permute-start.2
  604.4 7.3 collective-permute-start
  614.6 7.8 collective-permute-start.2
  628.6 7.3 collective-permute-start
  638.8 7.8 collective-permute-start.2
  663.1 7.8 collective-permute-start.2
  677.1 7.3 collective-permute-start
  687.3 7.8 collective-permute-start.2
  701.4 7.3 collective-permute-start
  711.5 7.8 collective-permute-start.2
  735.8 7.8 collective-permute-start.2
  749.8 7.3 collective-permute-start
  760.0 7.8 collective-permute-start.2
  784.3 7.8 collective-permute-start.2
  798.3 7.3 collective-permute-start
  808.5 7.8 collective-permute-start.2
  823.5 243.0 %all-gather.7.cloned.1.call-start = ((), (), s32[]{:S(2)}) async-start(), calls=%async_computation.1 | async-start | bytes 8454144 | tf_op jit(solution)/shard_map/all_gather | solution.py:114
  (73 other events, 720.6 us)
Sparse Core Ops, SparseCore 0:
  11.5 73.2 all-gather.4
  823.6 170.5 all-reduce.8
  997.8 68.6 all-gather.6
where the time goes:
time: 1090 us; the launch traced here: 1080 us
  waiting for transfers between devices  448 us (41%)
  starting transfers between devices  240 us (22%)
  local copies, waits for them, and re-layouts  200 us (18%)
  matrix products  118 us (11%)
  other arithmetic  38.7 us (4%)
  loops' own time  25.4 us (2%)
  between operations  13.9 us (1%)
    unnamed x4, waiting for transfers between devices  170 us
    ppermute x50, starting transfers between devices, with_halo(): lax.ppermute(lax.slice_in_dim(block, block.shape[dim] - width, None, axis...  159 us
    ppermute x50, waiting for transfers between devices, with_halo(): lax.ppermute(lax.slice_in_dim(block, 0, width, axis=dim), axis, backward)  133 us
    ppermute x50, starting transfers between devices, with_halo(): lax.ppermute(lax.slice_in_dim(block, 0, width, axis=dim), axis, backward)  80.5 us
    all_gather x1, waiting for transfers between devices, per_device(): lax.all_gather(flat_cells.astype(jnp.bfloat16), ('row', 'col'), axis=0, t...  74.4 us
    all_gather x1, waiting for transfers between devices, per_device(): lax.all_gather(updated, ('row', 'col'), axis=0, tiled=True)  70.4 us
    another operation x288, local copies, waits for them, and re-layouts, banded(): flat = jnp.tile(padded_taps, (1, size))[:, :size * (size + count - 1)]  59.6 us
    reshape x144, local copies, waits for them, and re-layouts, banded(): return flat.reshape(taps.shape[0], size, size + count - 1)  58.8 us
  transfers between devices with their start and end apart: 103, of which 29 were waited for; matrix products, arithmetic and copies ran while one was open for 6% of the time, Pallas kernels for 0%

commit v1 on v0

v1 whole, which is shorter than its diff:
```python
import jax
import jax.numpy as jnp
from jax import lax
from jax.experimental import pallas as pl
from jax.experimental.pallas import tpu as pltpu
from jax.sharding import PartitionSpec as P

AXES = ("row", "col")
ROWS, COLS = 4, 32
DEV = ROWS * COLS
BLK = 128
HALF = 17
WIN = BLK + 2 * HALF
TILE_R, TILE_C = 256, 384
EXT_R = 296
CHAN = 24
SLOTS = 16
BF, F32 = jnp.bfloat16, jnp.float32


def dot(a, b):
    return lax.dot_general(a, b, (((1,), (0,)), ((), ())), preferred_element_type=F32)


def iota(dim, shape=(DEV, BLK)):
    return lax.broadcasted_iota(jnp.int32, shape, dim)


def slot_ids(ids, holder):
    lane, dev = iota(1), iota(0)
    dev_row, dev_col = dev // COLS, dev % COLS
    upper = ids
    lower = pltpu.roll(ids, BLK - 3, 1)
    above = jnp.where(dev_row == 0, -1.0, pltpu.roll(lower, COLS, 0))
    below = jnp.where(dev_row == ROWS - 1, -1.0, pltpu.roll(upper, DEV - COLS, 0))
    third = jnp.where(holder >= BLK // 2, above, below)
    out = jnp.full((DEV, BLK), -1.0, F32)
    for p, part in enumerate((upper, lower, third)):
        left = jnp.where(dev_col == 0, -1.0, pltpu.roll(part, 1, 0))
        right = jnp.where(dev_col == COLS - 1, -1.0, pltpu.roll(part, DEV - 1, 0))
        here = pltpu.roll(part, 4 * p, 1) if p else part
        out = jnp.where((lane >= 4 * p) & (lane < 4 * p + 3), here, out)
        out = jnp.where(lane == 4 * p + 3, pltpu.roll(left, 4 * p + 1, 1), out)
        out = jnp.where(lane == 12 + p, pltpu.roll(right, 12 + p, 1), out)
    return out


def owner_select(owner_ref, transpose):
    if transpose:
        return (owner_ref[0:1, :] == iota(0)).astype(BF)
    return (owner_ref[...].T == iota(1)).astype(BF)


def columns_of(slots, s):
    return jnp.broadcast_to(slots[:, s : s + 1], (DEV, BLK))


def pick_kernel(holder_ref, table_ref, ids_ref, owner_ref, out_ref, held_ref, stage):
    lane = iota(1)
    slots = slot_ids(ids_ref[...].astype(F32), holder_ref[0])
    cell = lane.astype(F32)
    held = dot(owner_select(owner_ref, False), table_ref[...]).astype(BF)
    held_ref[...] = held

    def pick(s):
        return dot((columns_of(slots, s) == cell).astype(BF), held)

    for p in range(3):
        for q in range(3):
            stage[pl.ds(4 * p + q, DEV, stride=SLOTS), :] = pick(4 * p + q)
        halo = jnp.where(lane >= BLK // 2, pick(4 * p + 3), pick(12 + p))
        stage[pl.ds(4 * p + 3, DEV, stride=SLOTS), :] = halo
    for s in range(12, SLOTS):
        stage[pl.ds(s, DEV, stride=SLOTS), :] = jnp.zeros((DEV, BLK), F32)
    out_ref[...] = stage[...].astype(BF)


def toeplitz(taps_ref, m, shift_stride=1):
    base = jnp.broadcast_to(taps_ref[pl.ds(m, 1), :], (BLK, 2 * BLK))
    return pltpu.roll(base, 0, 1, stride=1, stride_axis=0).astype(BF)


def litho_kernel(
    weights_ref, recv_ref, target_ref, row_ref, row_rev_ref, col_ref, col_rev_ref,
    out_ref, stage, wide, mask, columns, field, light, grad, back_taps,
):
    stage[...] = recv_ref[...].astype(F32)
    for q in range(4):
        for p in range(3):
            wide[p * BLK : (p + 1) * BLK, q * BLK : (q + 1) * BLK] = stage[
                pl.ds(4 * p + q, DEV, stride=SLOTS), :
            ]
    mask[...] = pltpu.roll(pltpu.roll(wide[...], HALF, 1), HALF, 0)[:EXT_R].astype(BF)
    columns[:, EXT_R:, :] = jnp.zeros((2, 384 - EXT_R, TILE_C), BF)
    light[...] = jnp.zeros_like(light)

    def forward(k, carry):
        rolled = [toeplitz(col_rev_ref, 2 * k + r) for r in range(2)]
        col_matrix = jnp.concatenate(
            [
                jnp.concatenate([t[:, :BLK] for t in rolled], 1),
                jnp.concatenate([t[:, BLK:] for t in rolled], 1),
            ],
            0,
        )
        for q in range(3):
            made = dot(mask[:, q * BLK : (q + 2) * BLK], col_matrix).astype(BF)
            for r in range(2):
                columns[r, :EXT_R, q * BLK : (q + 1) * BLK] = made[:, r * BLK : (r + 1) * BLK]
        row_matrix = jnp.concatenate([toeplitz(row_ref, 2 * k + r) for r in range(2)], 1)
        weight = weights_ref[k // 2]
        for p in range(2):
            window = jnp.concatenate(
                [columns[r, p * BLK : (p + 2) * BLK, :] for r in range(2)], 0
            )
            made = dot(row_matrix, window)
            here = slice(p * BLK, (p + 1) * BLK)
            light[here] += weight * made * made
            field[k, here] = made
        return carry

    lax.fori_loop(0, CHAN, forward, 0)
    resist = jax.nn.sigmoid(3.0 * (light[...] - 1.3))
    light[...] = 2.0 * (resist - target_ref[...]) * 3.0 * resist * (1.0 - resist)
    grad[...] = jnp.zeros_like(grad)
    back_taps[...] = jnp.zeros_like(back_taps)

    def backward(k, carry):
        weighted = (2.0 * weights_ref[k // 2] * field[k] * light[...]).astype(BF)
        for r in range(2):
            rolled = toeplitz(row_rev_ref, 2 * k + r)
            top, bottom = rolled[:, :BLK], rolled[:, BLK:]
            at = r * EXT_R
            back_taps[at : at + BLK, :BLK] = top
            back_taps[at + BLK : at + 2 * BLK, BLK:] = top
            back_taps[at + BLK : at + 2 * BLK, :BLK] = bottom
            back_taps[at + 2 * BLK : at + EXT_R, BLK:] = bottom[: EXT_R - 2 * BLK]
        back = dot(back_taps[...], weighted).astype(BF)
        col_matrix = jnp.concatenate([toeplitz(col_ref, 2 * k + r) for r in range(2)], 0)
        for q in range(3):
            here = slice(q * BLK, (q + 1) * BLK)
            both = jnp.concatenate([back[:EXT_R, here], back[EXT_R:, here]], 1)
            grad[:EXT_R, q * BLK : (q + 2) * BLK] += dot(both, col_matrix)
        return carry

    lax.fori_loop(0, CHAN, backward, 0)
    wide[...] = pltpu.roll(pltpu.roll(grad[...], 384 - HALF, 0), 512 - HALF, 1)
    for q in range(4):
        for p in range(3):
            stage[pl.ds(4 * p + q, DEV, stride=SLOTS), :] = wide[
                p * BLK : (p + 1) * BLK, q * BLK : (q + 1) * BLK
            ]
    for s in range(12, SLOTS):
        stage[pl.ds(s, DEV, stride=SLOTS), :] = jnp.zeros((DEV, BLK), F32)
    out_ref[...] = stage[...].astype(BF)


def update_kernel(holder_ref, recv_ref, ids_ref, owner_ref, held_ref, out_ref, stage, out_stage):
    lane = iota(1)
    slots = slot_ids(ids_ref[...].astype(F32), holder_ref[0])
    slots_t = slots.T
    cell_down = iota(0).astype(F32)
    stage[...] = recv_ref[...].astype(F32)

    def gather(s, piece):
        select = (jnp.broadcast_to(slots_t[s : s + 1, :], (BLK, DEV)) == cell_down).astype(BF)
        return dot(select, stage[pl.ds(piece, DEV, stride=SLOTS), :].astype(BF))

    total = jnp.zeros((BLK, BLK), F32)
    from_left, from_right = total, total
    for p in range(3):
        for q in range(3):
            total += gather(4 * p + q, 4 * p + q)
        from_left += gather(4 * p + 3, 4 * p + 3)
        from_right += gather(12 + p, 4 * p + 3)
    total += jnp.where(lane >= BLK // 2, from_left, from_right)
    updated = (held_ref[...].astype(F32) - 0.05 * total).astype(BF)
    cell = lane.astype(F32)
    for p in range(2):
        for q in range(3):
            select = (columns_of(slots, 4 * p + q) == cell).astype(BF)
            out_stage[pl.ds(3 * p + q, DEV, stride=8), :] = dot(select, updated)
    by_owner = owner_select(owner_ref, True)
    out_stage[pl.ds(6, DEV, stride=8), :] = dot(by_owner, total.astype(BF))
    out_stage[pl.ds(7, DEV, stride=8), :] = jnp.zeros((DEV, BLK), F32)
    out_ref[...] = out_stage[...].astype(BF)


def unpack_kernel(recv_ref, grad_ref, mask_ref, stage):
    stage[...] = recv_ref[...].astype(F32)
    for p in range(2):
        for q in range(3):
            mask_ref[p * BLK : (p + 1) * BLK, q * BLK : (q + 1) * BLK] = stage[
                pl.ds(3 * p + q, DEV, stride=8), :
            ]
    grad_ref[...] = stage[pl.ds(6, DEV, stride=8), :]


SMEM = pl.BlockSpec(memory_space=pltpu.SMEM)
VMEM = pl.BlockSpec(memory_space=pltpu.VMEM)


def call(kernel, out_shape, in_specs, scratch, name):
    return pl.pallas_call(
        kernel,
        out_shape=out_shape,
        in_specs=in_specs,
        out_specs=jax.tree.map(lambda _: VMEM, out_shape),
        scratch_shapes=scratch,
        name=name,
    )


def exchange(x):
    return lax.all_to_all(x, AXES, 0, 0, tiled=True)


def per_device(cells, target, row_taps, col_taps, socs, cell_of_block, owner_map):
    struct = jax.ShapeDtypeStruct
    holder = (lax.axis_index("row") * COLS + lax.axis_index("col")).astype(jnp.int32).reshape(1)
    weights = socs / jnp.sum(socs)
    owner = jnp.broadcast_to(owner_map[None, :], (DEV, DEV))

    def spread(taps, reverse):
        flat = taps.reshape(2 * CHAN, 2 * HALF + 1).astype(F32)
        gap = jnp.zeros((2 * CHAN, 2 * BLK - 2 * HALF - 1), F32)
        if reverse:
            return jnp.concatenate([flat[:, :1], gap, flat[:, :0:-1]], 1)
        return jnp.concatenate([flat, gap], 1)

    own_ids = jnp.pad(cell_of_block.reshape(1, 6).astype(BF), ((0, 0), (0, BLK - 6)))
    first = jnp.stack([cells[0].astype(BF), jnp.broadcast_to(own_ids, (BLK, BLK))], 1)
    first = exchange(first)
    table, ids = first[:, 0], first[:, 1]

    picked, held = call(
        pick_kernel,
        (struct((DEV * SLOTS, BLK), BF), struct((BLK, BLK), BF)),
        [SMEM, VMEM, VMEM, VMEM],
        [pltpu.VMEM((DEV * SLOTS, BLK), F32)],
        "pick",
    )(holder, table, ids, owner)
    received = exchange(picked.reshape(DEV, SLOTS, BLK)).reshape(DEV * SLOTS, BLK)

    pieces = call(
        litho_kernel,
        struct((DEV * SLOTS, BLK), BF),
        [SMEM] + [VMEM] * 6,
        [
            pltpu.VMEM((DEV * SLOTS, BLK), F32),
            pltpu.VMEM((384, 512), F32),
            pltpu.VMEM((EXT_R, 512), BF),
            pltpu.VMEM((2, 384, TILE_C), BF),
            pltpu.VMEM((CHAN, TILE_R, TILE_C), F32),
            pltpu.VMEM((TILE_R, TILE_C), F32),
            pltpu.VMEM((384, 512), F32),
            pltpu.VMEM((2 * EXT_R, TILE_R), BF),
        ],
        "litho",
    )(
        weights, received, target,
        spread(row_taps, False), spread(row_taps, True),
        spread(col_taps, False), spread(col_taps, True),
    )
    pieces = exchange(pieces.reshape(DEV, SLOTS, BLK)).reshape(DEV * SLOTS, BLK)

    results = call(
        update_kernel,
        struct((DEV * 8, BLK), BF),
        [SMEM] + [VMEM] * 4,
        [pltpu.VMEM((DEV * SLOTS, BLK), F32), pltpu.VMEM((DEV * 8, BLK), F32)],
        "update",
    )(holder, pieces, ids, owner, held)
    results = exchange(results.reshape(DEV, 8, BLK)).reshape(DEV * 8, BLK)

    gradient, new_mask = call(
        unpack_kernel,
        (struct((BLK, BLK), F32), struct((TILE_R, TILE_C), F32)),
        [VMEM],
        [pltpu.VMEM((DEV * 8, BLK), F32)],
        "unpack",
    )(results)
    return gradient.reshape(1, BLK, BLK), new_mask


def solution(mesh):
    in_specs = (P(AXES, None, None), P("row", "col"), P(), P(), P(), P("row", "col"), P())
    out_specs = (P(AXES, None, None), P("row", "col"))
    return jax.shard_map(
        per_device, mesh=mesh, in_specs=in_specs, out_specs=out_specs, check_vma=False
    )
```

time: 1090 us -> 122 us (0.11)
  waiting for transfers between devices: 448 us -> 17.4 us
  starting transfers between devices: 240 us -> 16.1 us
  local copies, waits for them, and re-layouts: 200 us -> 6.52 us
  matrix products: 118 us -> 0 us
  Pallas kernels: 0 us -> 41.2 us
  blocking collectives: 0 us -> 35.6 us
  other arithmetic: 38.7 us -> 4.15 us
  loops' own time: 25.4 us -> 0 us
  between operations: 13.9 us -> 0.69 us
    ppermute x100 -> x0, starting transfers between devices: 240 us -> none  [the longest x50 159 us: with_halo(): lax.ppermute(lax.slice_in_dim(block, block.shape[dim] - width, None, axis...]
    unnamed x4 -> x0, waiting for transfers between devices: 170 us -> none
    all_gather x2 -> x0, waiting for transfers between devices: 145 us -> none  [the longest x1 74.4 us: per_device(): lax.all_gather(flat_cells.astype(jnp.bfloat16), ('row', 'col'), axis=0, t...]
    ppermute x100 -> x0, waiting for transfers between devices: 133 us -> none  [the longest x50 133 us: with_halo(): lax.ppermute(lax.slice_in_dim(block, 0, width, axis=dim), axis, backward)]
    dot_general x363 -> x0, matrix products: 118 us -> none  [the longest x216 55.3 us: separable(): jnp.einsum('ab,rcb->rac', window, col_matrix, preferred_element_type=jnp....]
    reshape x146 -> x0, local copies, waits for them, and re-layouts: 59.2 us -> none  [the longest x144 58.8 us: banded(): return flat.reshape(taps.shape[0], size, size + count - 1)]
    another operation x288 -> x3, local copies, waits for them, and re-layouts: 59.6 us -> 0.71 us  [the longest x2 0.7 us: per_device(): jnp.stack([cells[0].astype(BF), jnp.broadcast_to(own_ids, (BLK, BLK))], 1)]
    pallas_call x0 -> x4, Pallas kernels: none -> 41.2 us  [the longest x1 34 us: per_device(): call(litho_kernel, struct((DEV * SLOTS, BLK), BF), [SMEM] + [VMEM] * 6, [...]
  transfers between devices with their start and end apart: 103 -> 2, of which waited for: 29 -> 2; matrix products, arithmetic and copies ran while one was open for 6% -> 3% of each run, Pallas kernels for 0% -> 0%
where the time goes in v1:
time: 122 us
  Pallas kernels  41.2 us (34%)
  blocking collectives  35.6 us (29%)
  waiting for transfers between devices  17.4 us (14%)
  starting transfers between devices  16.1 us (13%)
  local copies, waits for them, and re-layouts  6.52 us (5%)
  other arithmetic  4.15 us (3%)
    all_to_all x2, blocking collectives, exchange(): return lax.all_to_all(x, AXES, 0, 0, tiled=True)  35.6 us
    pallas_call x1, Pallas kernels, per_device(): call(litho_kernel, struct((DEV * SLOTS, BLK), BF), [SMEM] + [VMEM] * 6, [...  34 us
    all_to_all x2, waiting for transfers between devices, exchange(): return lax.all_to_all(x, AXES, 0, 0, tiled=True)  17.4 us
    all_to_all x2, starting transfers between devices, exchange(): return lax.all_to_all(x, AXES, 0, 0, tiled=True)  16.1 us
    unnamed x10, local copies, waits for them, and re-layouts  2.73 us
    pallas_call x1, Pallas kernels, per_device(): call(update_kernel, struct((DEV * 8, BLK), BF), [SMEM] + [VMEM] * 4, [plt...  2.71 us
    pallas_call x1, Pallas kernels, per_device(): call(pick_kernel, (struct((DEV * SLOTS, BLK), BF), struct((BLK, BLK), BF)...  2.66 us
  transfers between devices with their start and end apart: 2, of which 2 were waited for; matrix products, arithmetic and copies ran while one was open for 3% of the time, Pallas kernels for 0%

profile of v1, /device:TPU:1, one launch (start us, length us, event | category | flops | bytes accessed | tf_op | source)
XLA Modules:
  0.0 121.6 jit_solution(2422885040253813491)
XLA Ops:
  0.6 0.7 convert_element_type.45
  1.3 0.1 convert_element_type.46
  1.4 0.8 convert_bitcast_fusion
  2.3 0.7 copy.11
  3.0 11.5 %all-to-all-start = ((bf16[128,2,128]{2,1,0:T(2,128)(2,1)}), bf16[128,2,128]{2,1,0:T(2,128)(2,1)S(1)}, u32[]{:S(2)}, u32[]{:S(2)}) async-start(bf16[128,2,128]{2,1,0:T(2,128)(2,1)} %copy.11), calls=%async_computation | async-start | bytes 131072 | tf_op jit(solution)/shard_map/all_to_all | solution.py:215
  14.5 9.4 %all-to-all-done = bf16[128,2,128]{2,1,0:T(2,128)(2,1)S(1)} async-done(((bf16[128,2,128]{2,1,0:T(2,128)(2,1)}), bf16[128,2,128]{2,1,0:T(2,128)(2,1)S(1)}, u32[]{:S(2)}, u32[]{:S(2)}) %all-to-all-start) | async-done | bytes 65568 | tf_op jit(solution)/shard_map/all_to_all | solution.py:215
  23.9 0.1 fusion
  24.0 0.6 copy_bitcast_fusion
  24.7 0.7 copy-done.3
  25.3 0.6 broadcast_in_dim.2.owner_ref
  25.9 2.7 %pick.1 = (bf16[2048,128]{1,0:T(8,128)(2,1)}, bf16[128,128]{1,0:T(8,128)(2,1)}) custom-call(s32[1]{0:T(128)} %bitcast.holder_ref, bf16[128,128]{1,0:T(8,128)(2,1)} %get-tuple-element.15.table_ref, bf16[128,128]{1,0:T(8,128)(2,1)} %get-tuple-element.14.ids_ref, s32[128,128]{1,0:T(8,128)} %broadcast_in_dim.2.owner_ref), custom_call_target="tpu_custom_call" | custom-call | tf_op jit(solution)/shard_map/pick/pallas_call | solution.py:236
  28.6 4.6 %all-to-all-start.1 = ((bf16[128,16,128]{2,1,0:T(8,128)(2,1)}), bf16[128,16,128]{2,1,0:T(8,128)(2,1)S(1)}, u32[]{:S(2)}, u32[]{:S(2)}) async-start(bf16[128,16,128]{2,1,0:T(8,128)(2,1)} %bitcast.25), calls=%async_computation.1 | async-start | bytes 1048576 | tf_op jit(solution)/shard_map/all_to_all | solution.py:215
  33.2 0.0 copy-done.1
  33.2 0.1 slice.27
  33.3 0.7 copy-done.2
  34.0 0.1 slice.29
  34.1 0.6 concatenate.12.row_ref
  34.7 0.6 concatenate.14.col_ref
  35.3 0.1 rev.6
  35.4 0.1 rev.7
  35.5 0.6 copy-done.4
  36.1 0.7 reduce_sum.9
  36.8 0.1 pad.14.clone
  36.8 1.2 %broadcast_divide_fusion.weights_ref = f32[12]{0:T(128)} fusion(f32[12]{0:T(128)S(1)} %copy-done.4, f32[]{:T(128)} %reduce_sum.9), kind=kLoop, calls=%fused_computation.7 | loop fusion | flops 12 | bytes 100 | tf_op jit(solution)/shard_map/div | solution.py:221
  38.1 0.7 pad_maximum_fusion.2
  38.8 7.9 %all-to-all-done.1 = bf16[128,16,128]{2,1,0:T(8,128)(2,1)S(1)} async-done(((bf16[128,16,128]{2,1,0:T(8,128)(2,1)}), bf16[128,16,128]{2,1,0:T(8,128)(2,1)S(1)}, u32[]{:S(2)}, u32[]{:S(2)}) %all-to-all-start.1) | async-done | bytes 524320 | tf_op jit(solution)/shard_map/all_to_all | solution.py:215
  46.7 0.8 copy-done
  47.5 34.0 %litho.1 = bf16[2048,128]{1,0:T(8,128)(2,1)} custom-call(f32[12]{0:T(128)} %broadcast_divide_fusion.weights_ref, bf16[2048,128]{1,0:T(8,128)(2,1)} %bitcast.20, f32[256,384]{1,0:T(8,128)} %target_ref.1, f32[48,256]{1,0:T(8,128)} %concatenate.12.row_ref, f32[48,256]{1,0:T(8,128)} %get-tuple-element.13.row_rev_ref, f32[48,256]{1,0:T(8,128)} %concatenate.14.col_ref, ...), custom_call_target="tpu_custom_call" | custom-call | tf_op jit(solution)/shard_map/litho/pallas_call | solution.py:245
  81.5 19.1 %all_to_all.20 = bf16[128,16,128]{2,1,0:T(8,128)(2,1)} all-to-all(bf16[128,16,128]{2,1,0:T(8,128)(2,1)} %bitcast.21), channel_id=1, replica_groups=mesh['row'=4,'col'=32] {'row','col'}, dimensions={0} | all-to-all | bytes 1048576 | tf_op jit(solution)/shard_map/all_to_all | solution.py:215
  100.5 2.7 %update.1 = bf16[1024,128]{1,0:T(8,128)(2,1)} custom-call(s32[1]{0:T(128)} %bitcast.holder_ref, bf16[2048,128]{1,0:T(8,128)(2,1)} %bitcast.22, bf16[128,128]{1,0:T(8,128)(2,1)} %get-tuple-element.14.ids_ref, s32[128,128]{1,0:T(8,128)} %broadcast_in_dim.2.owner_ref, bf16[128,128]{1,0:T(8,128)(2,1)} %get-tuple-element.7.held_ref), custom_call_target="tpu_custom_call" | custom-call | tf_op jit(solution)/shard_map/update/pallas_call | solution.py:267
  103.3 16.5 %all_to_all.21 = bf16[128,8,128]{2,1,0:T(8,128)(2,1)} all-to-all(bf16[128,8,128]{2,1,0:T(8,128)(2,1)} %bitcast.23), channel_id=1, replica_groups=mesh['row'=4,'col'=32] {'row','col'}, dimensions={0} | all-to-all | bytes 524288 | tf_op jit(solution)/shard_map/all_to_all | solution.py:215
  119.8 1.8 %unpack.1 = (f32[128,128]{1,0:T(8,128)}, f32[256,384]{1,0:T(8,128)}) custom-call(bf16[1024,128]{1,0:T(8,128)(2,1)} %bitcast.24), custom_call_target="tpu_custom_call" | custom-call | tf_op jit(solution)/shard_map/unpack/pallas_call | solution.py:276
  (11 shorter events, 0.0 us)
Async XLA Ops:
  3.0 20.9 %all-to-all-start = ((bf16[128,2,128]{2,1,0:T(2,128)(2,1)}), bf16[128,2,128]{2,1,0:T(2,128)(2,1)S(1)}, u32[]{:S(2)}, u32[]{:S(2)}) async-start(bf16[128,2,128]{2,1,0:T(2,128)(2,1)} %copy.11), calls=%async_computation | async-start | bytes 131072 | tf_op jit(solution)/shard_map/all_to_all | solution.py:215
  24.7 0.7 copy-start.3
  28.6 4.6 %copy-start.1 = (bf16[24,2,35]{2,1,0:T(2,128)(2,1)S(1)}, bf16[24,2,35]{2,1,0:T(2,128)(2,1)}, u32[]{:S(2)}) copy-start(bf16[24,2,35]{2,1,0:T(2,128)(2,1)} %param.9) | copy-start | bytes 10084
  28.6 18.1 %all-to-all-start.1 = ((bf16[128,16,128]{2,1,0:T(8,128)(2,1)}), bf16[128,16,128]{2,1,0:T(8,128)(2,1)S(1)}, u32[]{:S(2)}, u32[]{:S(2)}) async-start(bf16[128,16,128]{2,1,0:T(8,128)(2,1)} %bitcast.25), calls=%async_computation.1 | async-start | bytes 1048576 | tf_op jit(solution)/shard_map/all_to_all | solution.py:215
  33.3 0.7 copy-start.2
  35.4 0.7 copy-start.4
  46.7 0.8 copy-start

commit v2 on v1

--- a/solution.py
+++ b/solution.py
@@ -82,7 +82,7 @@
 
 def litho_kernel(
     weights_ref, recv_ref, target_ref, row_ref, row_rev_ref, col_ref, col_rev_ref,
-    out_ref, stage, wide, mask, columns, field, light, grad, back_taps,
+    out_ref, stage, wide, mask, columns_a, columns_b, field, light, grad, taps_a, taps_b, back_a, back_b,
 ):
     stage[...] = recv_ref[...].astype(F32)
     for q in range(4):
@@ -91,10 +91,11 @@
                 pl.ds(4 * p + q, DEV, stride=SLOTS), :
             ]
     mask[...] = pltpu.roll(pltpu.roll(wide[...], HALF, 1), HALF, 0)[:EXT_R].astype(BF)
-    columns[:, EXT_R:, :] = jnp.zeros((2, 384 - EXT_R, TILE_C), BF)
+    for columns in (columns_a, columns_b):
+        columns[:, EXT_R:, :] = jnp.zeros((2, 384 - EXT_R, TILE_C), BF)
     light[...] = jnp.zeros_like(light)
 
-    def forward(k, carry):
+    def make_columns(k, columns):
         rolled = [toeplitz(col_rev_ref, 2 * k + r) for r in range(2)]
         col_matrix = jnp.concatenate(
             [
@@ -107,6 +108,8 @@
             made = dot(mask[:, q * BLK : (q + 2) * BLK], col_matrix).astype(BF)
             for r in range(2):
                 columns[r, :EXT_R, q * BLK : (q + 1) * BLK] = made[:, r * BLK : (r + 1) * BLK]
+
+    def make_field(k, columns):
         row_matrix = jnp.concatenate([toeplitz(row_ref, 2 * k + r) for r in range(2)], 1)
         weight = weights_ref[k // 2]
         for p in range(2):
@@ -117,33 +120,62 @@
             here = slice(p * BLK, (p + 1) * BLK)
             light[here] += weight * made * made
             field[k, here] = made
+
+    make_columns(0, columns_a)
+
+    def forward(i, carry):
+        make_columns(2 * i + 1, columns_b)
+        make_field(2 * i, columns_a)
+        make_columns(jnp.minimum(2 * i + 2, CHAN - 1), columns_a)
+        make_field(2 * i + 1, columns_b)
         return carry
 
-    lax.fori_loop(0, CHAN, forward, 0)
+    lax.fori_loop(0, CHAN // 2, forward, 0)
     resist = jax.nn.sigmoid(3.0 * (light[...] - 1.3))
     light[...] = 2.0 * (resist - target_ref[...]) * 3.0 * resist * (1.0 - resist)
     grad[...] = jnp.zeros_like(grad)
-    back_taps[...] = jnp.zeros_like(back_taps)
-
-    def backward(k, carry):
+    for taps in (taps_a, taps_b):
+        taps[...] = jnp.zeros_like(taps)
+
+    def make_back(k, j, back):
+        taps = (taps_a, taps_b)[j]
         weighted = (2.0 * weights_ref[k // 2] * field[k] * light[...]).astype(BF)
         for r in range(2):
             rolled = toeplitz(row_rev_ref, 2 * k + r)
             top, bottom = rolled[:, :BLK], rolled[:, BLK:]
             at = r * EXT_R
-            back_taps[at : at + BLK, :BLK] = top
-            back_taps[at + BLK : at + 2 * BLK, BLK:] = top
-            back_taps[at + BLK : at + 2 * BLK, :BLK] = bottom
-            back_taps[at + 2 * BLK : at + EXT_R, BLK:] = bottom[: EXT_R - 2 * BLK]
-        back = dot(back_taps[...], weighted).astype(BF)
-        col_matrix = jnp.concatenate([toeplitz(col_ref, 2 * k + r) for r in range(2)], 0)
-        for q in range(3):
-            here = slice(q * BLK, (q + 1) * BLK)
-            both = jnp.concatenate([back[:EXT_R, here], back[EXT_R:, here]], 1)
-            grad[:EXT_R, q * BLK : (q + 2) * BLK] += dot(both, col_matrix)
+            taps[at : at + BLK, :BLK] = top
+            taps[at + BLK : at + 2 * BLK, BLK:] = top
+            taps[at + BLK : at + 2 * BLK, :BLK] = bottom
+            taps[at + 2 * BLK : at + EXT_R, BLK:] = bottom[: EXT_R - 2 * BLK]
+        made = dot(taps[...], weighted).astype(BF)
+        for r in range(2):
+            for q in range(3):
+                at = (4 * q + 2 * j + r) * BLK
+                back[:, at : at + BLK] = made[r * EXT_R : (r + 1) * EXT_R, q * BLK : (q + 1) * BLK]
+
+    def add_grad(k, back):
+        col_matrix = jnp.concatenate([toeplitz(col_ref, 2 * k + r) for r in range(4)], 0)
+        for q in range(3):
+            grad[:EXT_R, q * BLK : (q + 2) * BLK] += dot(
+                back[:, 4 * q * BLK : 4 * (q + 1) * BLK], col_matrix
+            )
+
+    make_back(0, 0, back_a)
+    make_back(1, 1, back_a)
+
+    def backward(i, carry):
+        k = 4 * i
+        make_back(k + 2, 0, back_b)
+        make_back(k + 3, 1, back_b)
+        add_grad(k, back_a)
+        later = jnp.minimum(k + 4, CHAN - 2)
+        make_back(later, 0, back_a)
+        make_back(later + 1, 1, back_a)
+        add_grad(k + 2, back_b)
         return carry
 
-    lax.fori_loop(0, CHAN, backward, 0)
+    lax.fori_loop(0, CHAN // 4, backward, 0)
     wide[...] = pltpu.roll(pltpu.roll(grad[...], 384 - HALF, 0), 512 - HALF, 1)
     for q in range(4):
         for p in range(3):
@@ -251,10 +283,14 @@
             pltpu.VMEM((384, 512), F32),
             pltpu.VMEM((EXT_R, 512), BF),
             pltpu.VMEM((2, 384, TILE_C), BF),
+            pltpu.VMEM((2, 384, TILE_C), BF),
             pltpu.VMEM((CHAN, TILE_R, TILE_C), F32),
             pltpu.VMEM((TILE_R, TILE_C), F32),
             pltpu.VMEM((384, 512), F32),
             pltpu.VMEM((2 * EXT_R, TILE_R), BF),
+            pltpu.VMEM((2 * EXT_R, TILE_R), BF),
+            pltpu.VMEM((EXT_R, 12 * BLK), BF),
+            pltpu.VMEM((EXT_R, 12 * BLK), BF),
         ],
         "litho",
     )(

time: 122 us -> 110 us (0.902)
  Pallas kernels: 41.2 us -> 28.9 us
    pallas_call x1, Pallas kernels: 34 us -> 21.7 us  [per_device(): call(litho_kernel, struct((DEV * SLOTS, BLK), BF), [SMEM] + [VMEM] * 6, [...]
  transfers between devices with their start and end apart: 2 -> 2, of which waited for: 2 -> 2; matrix products, arithmetic and copies ran while one was open for 3% -> 4% of each run, Pallas kernels for 0% -> 0%
where the time goes in v2:
time: 110 us; the launch traced here: 109 us
  blocking collectives  35.6 us (32%)
  Pallas kernels  28.9 us (26%)
  waiting for transfers between devices  17.4 us (16%)
  starting transfers between devices  16.1 us (15%)
  local copies, waits for them, and re-layouts  6.52 us (6%)
  other arithmetic  4.15 us (4%)
    all_to_all x2, blocking collectives, exchange(): return lax.all_to_all(x, AXES, 0, 0, tiled=True)  35.6 us
    pallas_call x1, Pallas kernels, per_device(): call(litho_kernel, struct((DEV * SLOTS, BLK), BF), [SMEM] + [VMEM] * 6, [...  21.7 us
    all_to_all x2, waiting for transfers between devices, exchange(): return lax.all_to_all(x, AXES, 0, 0, tiled=True)  17.4 us
    all_to_all x2, starting transfers between devices, exchange(): return lax.all_to_all(x, AXES, 0, 0, tiled=True)  16.1 us
    unnamed x10, local copies, waits for them, and re-layouts  2.73 us
    pallas_call x1, Pallas kernels, per_device(): call(update_kernel, struct((DEV * 8, BLK), BF), [SMEM] + [VMEM] * 4, [plt...  2.71 us
    pallas_call x1, Pallas kernels, per_device(): call(pick_kernel, (struct((DEV * SLOTS, BLK), BF), struct((BLK, BLK), BF)...  2.66 us
  transfers between devices with their start and end apart: 2, of which 2 were waited for; matrix products, arithmetic and copies ran while one was open for 4% of the time, Pallas kernels for 0%

profile of v2, /device:TPU:1, one launch (start us, length us, event | category | flops | bytes accessed | tf_op | source)
XLA Modules:
  0.0 109.3 jit_solution(4004385862003680773)
XLA Ops:
  0.6 0.7 convert_element_type.45
  1.3 0.1 convert_element_type.46
  1.4 0.8 convert_bitcast_fusion
  2.3 0.7 copy.11
  3.0 11.5 %all-to-all-start = ((bf16[128,2,128]{2,1,0:T(2,128)(2,1)}), bf16[128,2,128]{2,1,0:T(2,128)(2,1)S(1)}, u32[]{:S(2)}, u32[]{:S(2)}) async-start(bf16[128,2,128]{2,1,0:T(2,128)(2,1)} %copy.11), calls=%async_computation | async-start | bytes 131072 | tf_op jit(solution)/shard_map/all_to_all | solution.py:247
  14.5 9.4 %all-to-all-done = bf16[128,2,128]{2,1,0:T(2,128)(2,1)S(1)} async-done(((bf16[128,2,128]{2,1,0:T(2,128)(2,1)}), bf16[128,2,128]{2,1,0:T(2,128)(2,1)S(1)}, u32[]{:S(2)}, u32[]{:S(2)}) %all-to-all-start) | async-done | bytes 65568 | tf_op jit(solution)/shard_map/all_to_all | solution.py:247
  23.9 0.1 fusion
  24.0 0.6 copy_bitcast_fusion
  24.7 0.7 copy-done.3
  25.3 0.6 broadcast_in_dim.2.owner_ref
  25.9 2.7 %pick.1 = (bf16[2048,128]{1,0:T(8,128)(2,1)}, bf16[128,128]{1,0:T(8,128)(2,1)}) custom-call(s32[1]{0:T(128)} %bitcast.holder_ref, bf16[128,128]{1,0:T(8,128)(2,1)} %get-tuple-element.15.table_ref, bf16[128,128]{1,0:T(8,128)(2,1)} %get-tuple-element.14.ids_ref, s32[128,128]{1,0:T(8,128)} %broadcast_in_dim.2.owner_ref), custom_call_target="tpu_custom_call" | custom-call | tf_op jit(solution)/shard_map/pick/pallas_call | solution.py:268
  28.6 4.6 %all-to-all-start.1 = ((bf16[128,16,128]{2,1,0:T(8,128)(2,1)}), bf16[128,16,128]{2,1,0:T(8,128)(2,1)S(1)}, u32[]{:S(2)}, u32[]{:S(2)}) async-start(bf16[128,16,128]{2,1,0:T(8,128)(2,1)} %bitcast.25), calls=%async_computation.1 | async-start | bytes 1048576 | tf_op jit(solution)/shard_map/all_to_all | solution.py:247
  33.2 0.0 copy-done.1
  33.2 0.1 slice.27
  33.3 0.7 copy-done.2
  34.0 0.1 slice.29
  34.1 0.6 concatenate.12.row_ref
  34.7 0.6 concatenate.14.col_ref
  35.3 0.1 rev.6
  35.4 0.1 rev.7
  35.5 0.6 copy-done.4
  36.1 0.7 reduce_sum.9
  36.8 0.1 pad.14.clone
  36.8 1.2 %broadcast_divide_fusion.weights_ref = f32[12]{0:T(128)} fusion(f32[12]{0:T(128)S(1)} %copy-done.4, f32[]{:T(128)} %reduce_sum.9), kind=kLoop, calls=%fused_computation.7 | loop fusion | flops 12 | bytes 100 | tf_op jit(solution)/shard_map/div | solution.py:253
  38.1 0.7 pad_maximum_fusion.2
  38.8 7.9 %all-to-all-done.1 = bf16[128,16,128]{2,1,0:T(8,128)(2,1)S(1)} async-done(((bf16[128,16,128]{2,1,0:T(8,128)(2,1)}), bf16[128,16,128]{2,1,0:T(8,128)(2,1)S(1)}, u32[]{:S(2)}, u32[]{:S(2)}) %all-to-all-start.1) | async-done | bytes 524320 | tf_op jit(solution)/shard_map/all_to_all | solution.py:247
  46.7 0.8 copy-done
  47.5 21.7 %litho.1 = bf16[2048,128]{1,0:T(8,128)(2,1)} custom-call(f32[12]{0:T(128)} %broadcast_divide_fusion.weights_ref, bf16[2048,128]{1,0:T(8,128)(2,1)} %bitcast.20, f32[256,384]{1,0:T(8,128)} %target_ref.1, f32[48,256]{1,0:T(8,128)} %concatenate.12.row_ref, f32[48,256]{1,0:T(8,128)} %get-tuple-element.13.row_rev_ref, f32[48,256]{1,0:T(8,128)} %concatenate.14.col_ref, ...), custom_call_target="tpu_custom_call" | custom-call | tf_op jit(solution)/shard_map/litho/pallas_call | solution.py:277
  69.2 19.1 %all_to_all.20 = bf16[128,16,128]{2,1,0:T(8,128)(2,1)} all-to-all(bf16[128,16,128]{2,1,0:T(8,128)(2,1)} %bitcast.21), channel_id=1, replica_groups=mesh['row'=4,'col'=32] {'row','col'}, dimensions={0} | all-to-all | bytes 1048576 | tf_op jit(solution)/shard_map/all_to_all | solution.py:247
  88.3 2.7 %update.1 = bf16[1024,128]{1,0:T(8,128)(2,1)} custom-call(s32[1]{0:T(128)} %bitcast.holder_ref, bf16[2048,128]{1,0:T(8,128)(2,1)} %bitcast.22, bf16[128,128]{1,0:T(8,128)(2,1)} %get-tuple-element.14.ids_ref, s32[128,128]{1,0:T(8,128)} %broadcast_in_dim.2.owner_ref, bf16[128,128]{1,0:T(8,128)(2,1)} %get-tuple-element.7.held_ref), custom_call_target="tpu_custom_call" | custom-call | tf_op jit(solution)/shard_map/update/pallas_call | solution.py:303
  91.0 16.5 %all_to_all.21 = bf16[128,8,128]{2,1,0:T(8,128)(2,1)} all-to-all(bf16[128,8,128]{2,1,0:T(8,128)(2,1)} %bitcast.23), channel_id=1, replica_groups=mesh['row'=4,'col'=32] {'row','col'}, dimensions={0} | all-to-all | bytes 524288 | tf_op jit(solution)/shard_map/all_to_all | solution.py:247
  107.5 1.8 %unpack.1 = (f32[128,128]{1,0:T(8,128)}, f32[256,384]{1,0:T(8,128)}) custom-call(bf16[1024,128]{1,0:T(8,128)(2,1)} %bitcast.24), custom_call_target="tpu_custom_call" | custom-call | tf_op jit(solution)/shard_map/unpack/pallas_call | solution.py:312
  (11 shorter events, 0.0 us)
Async XLA Ops:
  3.0 20.9 %all-to-all-start = ((bf16[128,2,128]{2,1,0:T(2,128)(2,1)}), bf16[128,2,128]{2,1,0:T(2,128)(2,1)S(1)}, u32[]{:S(2)}, u32[]{:S(2)}) async-start(bf16[128,2,128]{2,1,0:T(2,128)(2,1)} %copy.11), calls=%async_computation | async-start | bytes 131072 | tf_op jit(solution)/shard_map/all_to_all | solution.py:247
  24.7 0.7 copy-start.3
  28.6 4.6 %copy-start.1 = (bf16[24,2,35]{2,1,0:T(2,128)(2,1)S(1)}, bf16[24,2,35]{2,1,0:T(2,128)(2,1)}, u32[]{:S(2)}) copy-start(bf16[24,2,35]{2,1,0:T(2,128)(2,1)} %param.9) | copy-start | bytes 10084
  28.6 18.1 %all-to-all-start.1 = ((bf16[128,16,128]{2,1,0:T(8,128)(2,1)}), bf16[128,16,128]{2,1,0:T(8,128)(2,1)S(1)}, u32[]{:S(2)}, u32[]{:S(2)}) async-start(bf16[128,16,128]{2,1,0:T(8,128)(2,1)} %bitcast.25), calls=%async_computation.1 | async-start | bytes 1048576 | tf_op jit(solution)/shard_map/all_to_all | solution.py:247
  33.3 0.7 copy-start.2
  35.4 0.7 copy-start.4
  46.7 0.8 copy-start

commit v3 on v2

v3 whole, which is shorter than its diff:
```python
import jax
import jax.numpy as jnp
from jax import lax
from jax.experimental import pallas as pl
from jax.experimental.pallas import tpu as pltpu
from jax.sharding import PartitionSpec as P

AXES = ("row", "col")
ROWS, COLS = 4, 32
DEV = ROWS * COLS
BLK = 128
HALF = 17
WIN = BLK + 2 * HALF
TILE_R, TILE_C = 256, 384
EXT_R = 296
TAIL = 48
CHAN = 24
SLOTS = 16
PER_COL = 12 * ROWS
BF, F32 = jnp.bfloat16, jnp.float32


def dot(a, b):
    return lax.dot_general(a, b, (((1,), (0,)), ((), ())), preferred_element_type=F32)


def iota(dim, shape=(DEV, BLK)):
    return lax.broadcasted_iota(jnp.int32, shape, dim)


def slot_ids(ids, holder_col):
    lane, dev = iota(1), iota(0)
    dev_row, dev_col = dev // COLS, dev % COLS
    upper = ids
    lower = pltpu.roll(ids, BLK - 3, 1)
    above = jnp.where(dev_row == 0, -1.0, pltpu.roll(lower, COLS, 0))
    below = jnp.where(dev_row == ROWS - 1, -1.0, pltpu.roll(upper, DEV - COLS, 0))
    third = jnp.where(holder_col >= COLS // 2, above, below)
    out = jnp.full((DEV, BLK), -1.0, F32)
    for p, part in enumerate((upper, lower, third)):
        left = jnp.where(dev_col == 0, -1.0, pltpu.roll(part, 1, 0))
        right = jnp.where(dev_col == COLS - 1, -1.0, pltpu.roll(part, DEV - 1, 0))
        here = pltpu.roll(part, 4 * p, 1) if p else part
        out = jnp.where((lane >= 4 * p) & (lane < 4 * p + 3), here, out)
        out = jnp.where(lane == 4 * p + 3, pltpu.roll(left, 4 * p + 1, 1), out)
        out = jnp.where(lane == 12 + p, pltpu.roll(right, 12 + p, 1), out)
    return out


def owner_select(owner_ref, transpose):
    owner = jnp.broadcast_to(owner_ref[...], (DEV, DEV))
    if transpose:
        return (owner == iota(0)).astype(BF)
    return (owner.astype(F32).T == iota(1).astype(F32)).astype(BF)


def columns_of(slots, s):
    return jnp.broadcast_to(slots[:, s : s + 1], (slots.shape[0], BLK))


def pack_kernel(blocks_ref, cells_ref, out_ref, stage):
    lane = iota(1, (COLS, BLK))
    ids = jnp.full((COLS, BLK), -1.0, F32)
    for n in range(6):
        ids = jnp.where(lane == n, blocks_ref[n // 3, n % 3].astype(F32), ids)
    for s in range(ROWS):
        stage[pl.ds(s, COLS, stride=8), :] = cells_ref[pl.ds(s, COLS, stride=ROWS), :]
    stage[pl.ds(ROWS, COLS, stride=8), :] = ids
    for s in range(ROWS + 1, 8):
        stage[pl.ds(s, COLS, stride=8), :] = jnp.zeros((COLS, BLK), F32)
    packed = stage[...].astype(BF)
    for r in range(ROWS):
        out_ref[r * COLS * 8 : (r + 1) * COLS * 8, :] = packed


def pick_kernel(place_ref, first_ref, owner_ref, out_ref, held_ref, slots_ref, stage, mine, out_stage):
    stage[...] = first_ref[...].astype(F32)
    slots = slot_ids(stage[pl.ds(ROWS, DEV, stride=8), :], place_ref[1])
    slots_ref[...] = slots
    table = jnp.concatenate([stage[pl.ds(s, DEV, stride=8), :] for s in range(ROWS)], 1)
    held = dot(owner_select(owner_ref, False), table.astype(BF)).astype(BF)
    row = place_ref[0]
    own = held[:, :BLK].astype(F32)
    for s in range(1, ROWS):
        own = jnp.where(row == s, held[:, s * BLK : (s + 1) * BLK].astype(F32), own)
    held_ref[...] = own
    mine[...] = slots_ref[pl.ds(pl.multiple_of(row * COLS, COLS), COLS), :]
    here = mine[...]
    cell = iota(1, (COLS, BLK)).astype(F32)
    select = jnp.concatenate([(columns_of(here, s) == cell).astype(BF) for s in range(15)], 0)
    picked = dot(select, held)
    wide_lane = iota(1, (COLS, ROWS * BLK)) % BLK
    for t in range(12):
        made = picked[t * COLS : (t + 1) * COLS]
        if t % 4 == 3:
            at = (12 + t // 4) * COLS
            made = jnp.where(wide_lane >= BLK // 2, made, picked[at : at + COLS])
        for s in range(ROWS):
            out_stage[pl.ds(ROWS * t + s, COLS, stride=PER_COL), :] = made[:, s * BLK : (s + 1) * BLK]
    out_ref[...] = out_stage[...].astype(BF)


def toeplitz(taps_ref, m):
    base = jnp.broadcast_to(taps_ref[pl.ds(m, 1), :], (BLK, 2 * BLK))
    return pltpu.roll(base, 0, 1, stride=1, stride_axis=0).astype(BF)


def litho_kernel(
    weights_ref, recv_ref, target_ref, row_ref, row_rev_ref, col_ref, col_rev_ref,
    out_ref, stage, wide, mask, columns_a, columns_b, field, light, grad, back_a, back_b,
):
    stage[: COLS * PER_COL, :] = recv_ref[...].astype(F32)
    for q in range(4):
        for p in range(3):
            for s in range(ROWS):
                wide[q, pl.ds(p * BLK + s, COLS, stride=ROWS), :] = stage[
                    pl.ds(ROWS * (4 * p + q) + s, COLS, stride=PER_COL), :
                ]
    whole = jnp.concatenate([wide[q] for q in range(4)], 1)
    mask[...] = pltpu.roll(pltpu.roll(whole, HALF, 1), HALF, 0)[:EXT_R].astype(BF)
    for columns in (columns_a, columns_b):
        columns[:, EXT_R:, :] = jnp.zeros((2, 384 - EXT_R, TILE_C), BF)
    light[...] = jnp.zeros_like(light)

    def make_columns(k, columns):
        rolled = [toeplitz(col_rev_ref, 2 * k + r) for r in range(2)]
        col_matrix = jnp.concatenate(
            [
                jnp.concatenate([t[:, :BLK] for t in rolled], 1),
                jnp.concatenate([t[:, BLK:] for t in rolled], 1),
            ],
            0,
        )
        for q in range(3):
            made = dot(mask[:, q * BLK : (q + 2) * BLK], col_matrix).astype(BF)
            for r in range(2):
                columns[r, :EXT_R, q * BLK : (q + 1) * BLK] = made[:, r * BLK : (r + 1) * BLK]

    def make_field(k, columns):
        row_matrix = jnp.concatenate([toeplitz(row_ref, 2 * k + r) for r in range(2)], 1)
        weight = weights_ref[k // 2]
        windows = [
            jnp.concatenate([columns[r, p * BLK : (p + 2) * BLK, :] for r in range(2)], 0)
            for p in range(2)
        ]
        last = dot(row_matrix, jnp.concatenate([w[:, 2 * BLK :] for w in windows], 1))
        for p in range(2):
            made = jnp.concatenate(
                [dot(row_matrix, windows[p][:, : 2 * BLK]), last[:, p * BLK : (p + 1) * BLK]], 1
            )
            here = slice(p * BLK, (p + 1) * BLK)
            light[here] += weight * made * made
            field[k, here] = made

    make_columns(0, columns_a)

    def forward(i, carry):
        make_columns(2 * i + 1, columns_b)
        make_field(2 * i, columns_a)
        make_columns(jnp.minimum(2 * i + 2, CHAN - 1), columns_a)
        make_field(2 * i + 1, columns_b)
        return carry

    lax.fori_loop(0, CHAN // 2, forward, 0)
    resist = jax.nn.sigmoid(3.0 * (light[...] - 1.3))
    light[...] = 2.0 * (resist - target_ref[...]) * 3.0 * resist * (1.0 - resist)
    grad[...] = jnp.zeros_like(grad)

    def make_back(k, j, back):
        weight = 2.0 * weights_ref[k // 2]
        upper, lower = [
            (weight * field[k, p * BLK : (p + 1) * BLK] * light[p * BLK : (p + 1) * BLK]).astype(BF)
            for p in range(2)
        ]
        rolled = [toeplitz(row_rev_ref, 2 * k + r) for r in range(2)]
        both = jnp.concatenate(rolled, 0)
        tail = jnp.concatenate([t[:TAIL, BLK:] for t in rolled], 0)
        second = jnp.concatenate([lower, upper], 0)
        first = jnp.concatenate([upper, jnp.zeros_like(upper)], 0)
        last = dot(both, jnp.concatenate([first[:, 2 * BLK :], second[:, 2 * BLK :]], 1)).astype(BF)
        parts = [
            dot(both[:, :BLK], upper[:, : 2 * BLK]).astype(BF),
            dot(both, second[:, : 2 * BLK]).astype(BF),
        ]
        end = dot(tail, lower).astype(BF)
        for r in range(2):
            for q in range(3):
                at = (4 * q + 2 * j + r) * BLK
                for p in range(2):
                    piece = last if q == 2 else parts[p]
                    lanes = p * BLK if q == 2 else q * BLK
                    back[p * BLK : (p + 1) * BLK, at : at + BLK] = piece[
                        r * BLK : (r + 1) * BLK, lanes : lanes + BLK
                    ]
                back[2 * BLK :, at : at + BLK] = end[
                    r * TAIL : r * TAIL + EXT_R - 2 * BLK, q * BLK : (q + 1) * BLK
                ]

    def add_grad(k, back):
        col_matrix = jnp.concatenate([toeplitz(col_ref, 2 * k + r) for r in range(4)], 0)
        for q in range(3):
            grad[:EXT_R, q * BLK : (q + 2) * BLK] += dot(
                back[:, 4 * q * BLK : 4 * (q + 1) * BLK], col_matrix
            )

    make_back(0, 0, back_a)
    make_back(1, 1, back_a)

    def backward(i, carry):
        k = 4 * i
        make_back(k + 2, 0, back_b)
        make_back(k + 3, 1, back_b)
        add_grad(k, back_a)
        later = jnp.minimum(k + 4, CHAN - 2)
        make_back(later, 0, back_a)
        make_back(later + 1, 1, back_a)
        add_grad(k + 2, back_b)
        return carry

    lax.fori_loop(0, CHAN // 4, backward, 0)
    whole = pltpu.roll(pltpu.roll(grad[...], 384 - HALF, 0), 512 - HALF, 1)
    for q in range(4):
        wide[q] = whole[:, q * BLK : (q + 1) * BLK]
    for q in range(4):
        for p in range(3):
            for r in range(ROWS):
                stage[pl.ds(r * COLS * SLOTS + 4 * p + q, COLS, stride=SLOTS), :] = wide[
                    q, pl.ds(p * BLK + r, COLS, stride=ROWS), :
                ]
    for s in range(12, SLOTS):
        stage[pl.ds(s, DEV, stride=SLOTS), :] = jnp.zeros((DEV, BLK), F32)
    out_ref[...] = stage[...].astype(BF)


def update_kernel(recv_ref, slots_ref, owner_ref, held_ref, out_ref, stage, out_stage):
    lane = iota(1)
    slots = slots_ref[...]
    slots_t = slots.T
    cell_down = iota(0).astype(F32)
    stage[...] = recv_ref[...].astype(F32)

    def gather(s, piece):
        select = (jnp.broadcast_to(slots_t[s : s + 1, :], (BLK, DEV)) == cell_down).astype(BF)
        return dot(select, stage[pl.ds(piece, DEV, stride=SLOTS), :].astype(BF))

    total = jnp.zeros((BLK, BLK), F32)
    from_left, from_right = total, total
    for p in range(3):
        for q in range(3):
            total += gather(4 * p + q, 4 * p + q)
        from_left += gather(4 * p + 3, 4 * p + 3)
        from_right += gather(12 + p, 4 * p + 3)
    total += jnp.where(lane >= BLK // 2, from_left, from_right)
    updated = (held_ref[...] - 0.05 * total).astype(BF)
    cell = lane.astype(F32)
    for p in range(2):
        for q in range(3):
            select = (columns_of(slots, 4 * p + q) == cell).astype(BF)
            out_stage[pl.ds(3 * p + q, DEV, stride=8), :] = dot(select, updated)
    by_owner = owner_select(owner_ref, True)
    out_stage[pl.ds(6, DEV, stride=8), :] = dot(by_owner, total.astype(BF))
    out_stage[pl.ds(7, DEV, stride=8), :] = jnp.zeros((DEV, BLK), F32)
    out_ref[...] = out_stage[...].astype(BF)


def unpack_kernel(recv_ref, grad_ref, mask_ref, stage, wide):
    stage[...] = recv_ref[...].astype(F32)
    for r in range(ROWS):
        for p in range(2):
            for q in range(3):
                wide[q, pl.ds(p * BLK + r, COLS, stride=ROWS), :] = stage[
                    pl.ds(r * COLS * 8 + 3 * p + q, COLS, stride=8), :
                ]
        grad_ref[pl.ds(r, COLS, stride=ROWS), :] = stage[pl.ds(r * COLS * 8 + 6, COLS, stride=8), :]
    for q in range(3):
        mask_ref[:, q * BLK : (q + 1) * BLK] = wide[q]


SMEM = pl.BlockSpec(memory_space=pltpu.SMEM)
VMEM = pl.BlockSpec(memory_space=pltpu.VMEM)


def call(kernel, out_shape, in_specs, scratch, name, limit=8):
    return pl.pallas_call(
        kernel,
        out_shape=out_shape,
        in_specs=in_specs,
        out_specs=jax.tree.map(lambda _: VMEM, out_shape),
        scratch_shapes=scratch,
        name=name,
        compiler_params=pltpu.CompilerParams(vmem_limit_bytes=limit << 20),
    )


def exchange(x, axes=AXES):
    return lax.all_to_all(x, axes, 0, 0, tiled=True)


def per_device(cells, target, row_taps, col_taps, socs, cell_of_block, owner_map):
    struct = jax.ShapeDtypeStruct
    place = jnp.stack([lax.axis_index("row"), lax.axis_index("col")]).astype(jnp.int32)
    weights = socs / jnp.sum(socs)
    owner = owner_map.reshape(1, DEV)

    def spread(taps, reverse):
        flat = taps.reshape(2 * CHAN, 2 * HALF + 1).astype(F32)
        gap = jnp.zeros((2 * CHAN, 2 * BLK - 2 * HALF - 1), F32)
        if reverse:
            return jnp.concatenate([flat[:, :1], gap, flat[:, :0:-1]], 1)
        return jnp.concatenate([flat, gap], 1)

    first = call(
        pack_kernel,
        struct((DEV * 8, BLK), BF),
        [SMEM, VMEM],
        [pltpu.VMEM((COLS * 8, BLK), F32)],
        "pack",
    )(cell_of_block, cells.reshape(BLK, BLK))
    first = exchange(first.reshape(DEV, 8, BLK)).reshape(DEV * 8, BLK)

    picked, held, slots = call(
        pick_kernel,
        (struct((COLS * PER_COL, BLK), BF), struct((BLK, BLK), F32), struct((DEV, BLK), F32)),
        [SMEM, VMEM, VMEM],
        [
            pltpu.VMEM((DEV * 8, BLK), F32),
            pltpu.VMEM((COLS, BLK), F32),
            pltpu.VMEM((COLS * PER_COL, BLK), F32),
        ],
        "pick",
    )(place, first, owner)
    received = exchange(picked.reshape(COLS, PER_COL, BLK), "col").reshape(COLS * PER_COL, BLK)

    pieces = call(
        litho_kernel,
        struct((DEV * SLOTS, BLK), BF),
        [SMEM] + [VMEM] * 6,
        [
            pltpu.VMEM((DEV * SLOTS, BLK), F32),
            pltpu.VMEM((4, 384, BLK), F32),
            pltpu.VMEM((EXT_R, 512), BF),
            pltpu.VMEM((2, 384, TILE_C), BF),
            pltpu.VMEM((2, 384, TILE_C), BF),
            pltpu.VMEM((CHAN, TILE_R, TILE_C), F32),
            pltpu.VMEM((TILE_R, TILE_C), F32),
            pltpu.VMEM((384, 512), F32),
            pltpu.VMEM((EXT_R, 12 * BLK), BF),
            pltpu.VMEM((EXT_R, 12 * BLK), BF),
        ],
        "litho",
        32,
    )(
        weights, received, target,
        spread(row_taps, False), spread(row_taps, True),
        spread(col_taps, False), spread(col_taps, True),
    )
    pieces = exchange(pieces.reshape(DEV, SLOTS, BLK)).reshape(DEV * SLOTS, BLK)

    results = call(
        update_kernel,
        struct((DEV * 8, BLK), BF),
        [VMEM] * 4,
        [pltpu.VMEM((DEV * SLOTS, BLK), F32), pltpu.VMEM((DEV * 8, BLK), F32)],
        "update",
    )(pieces, slots, owner, held)
    results = exchange(results.reshape(DEV, 8, BLK)).reshape(DEV * 8, BLK)

    gradient, new_mask = call(
        unpack_kernel,
        (struct((BLK, BLK), F32), struct((TILE_R, TILE_C), F32)),
        [VMEM],
        [pltpu.VMEM((DEV * 8, BLK), F32), pltpu.VMEM((3, TILE_R, BLK), F32)],
        "unpack",
    )(results)
    return gradient.reshape(1, BLK, BLK), new_mask


def solution(mesh):
    in_specs = (P(AXES, None, None), P("row", "col"), P(), P(), P(), P("row", "col"), P())
    out_specs = (P(AXES, None, None), P("row", "col"))
    return jax.shard_map(
        per_device, mesh=mesh, in_specs=in_specs, out_specs=out_specs, check_vma=False
    )
```

time: 110 us -> 97 us (0.88)
  Pallas kernels: 28.9 us -> 23.9 us
  blocking collectives: 35.6 us -> 32.5 us
  other arithmetic: 4.15 us -> 1.41 us
  local copies, waits for them, and re-layouts: 6.52 us -> 3.92 us
    all_to_all x2, blocking collectives: 35.6 us -> 32.5 us  [exchange(): return lax.all_to_all(x, axes, 0, 0, tiled=True)]
    pallas_call x1, Pallas kernels: 21.7 us -> 18.9 us  [per_device(): call(litho_kernel, struct((DEV * SLOTS, BLK), BF), [SMEM] + [VMEM] * 6, [...]
    convert_element_type x2 -> x0, other arithmetic: 1.53 us -> none  [the longest x1 0.84 us: per_device(): cells[0].astype(BF)]
    pallas_call x2 -> x3, Pallas kernels: 5.37 us -> 4.12 us  [the longest x1 2.06 us: per_device(): call(pick_kernel, (struct((COLS * PER_COL, BLK), BF), struct((BLK, BLK),...]
    concatenate x2, local copies, waits for them, and re-layouts: 1.25 us -> 0.01 us  [spread(): return jnp.concatenate([flat, gap], 1)]
    unnamed x10 -> x14, local copies, waits for them, and re-layouts: 2.73 us -> 3.53 us
  transfers between devices with their start and end apart: 2 -> 2, of which waited for: 2 -> 2; matrix products, arithmetic and copies ran while one was open for 4% -> 2% of each run, Pallas kernels for 0% -> 0%
where the time goes in v3:
time: 97 us; the launch traced here: 96.5 us
  blocking collectives  32.5 us (34%)
  Pallas kernels  23.9 us (25%)
  waiting for transfers between devices  17.7 us (18%)
  starting transfers between devices  16.3 us (17%)
  local copies, waits for them, and re-layouts  3.92 us (4%)
  other arithmetic  1.41 us (1%)
    all_to_all x2, blocking collectives, exchange(): return lax.all_to_all(x, axes, 0, 0, tiled=True)  32.5 us
    pallas_call x1, Pallas kernels, per_device(): call(litho_kernel, struct((DEV * SLOTS, BLK), BF), [SMEM] + [VMEM] * 6, [...  18.9 us
    all_to_all x2, waiting for transfers between devices, exchange(): return lax.all_to_all(x, axes, 0, 0, tiled=True)  17.7 us
    all_to_all x2, starting transfers between devices, exchange(): return lax.all_to_all(x, axes, 0, 0, tiled=True)  16.3 us
    unnamed x14, local copies, waits for them, and re-layouts  3.53 us
    pallas_call x1, Pallas kernels, per_device(): call(pick_kernel, (struct((COLS * PER_COL, BLK), BF), struct((BLK, BLK),...  2.06 us
  transfers between devices with their start and end apart: 2, of which 2 were waited for; matrix products, arithmetic and copies ran while one was open for 2% of the time, Pallas kernels for 0%

profile of v3, /device:TPU:1, one launch (start us, length us, event | category | flops | bytes accessed | tf_op | source)
XLA Modules:
  0.0 96.5 jit_solution(442735077025132368)
XLA Ops:
  0.6 0.0 copy-start.3
  0.6 0.7 copy-done.3
  1.3 0.0 copy-start.1
  1.3 0.8 copy-done.1
  2.1 1.3 %pack.1 = bf16[1024,128]{1,0:T(8,128)(2,1)} custom-call(s32[2,3]{1,0:T(2,128)S(1)} %copy-done.3, f32[128,128]{1,0:T(8,128)S(1)} %bitcast.23), custom_call_target="tpu_custom_call" | custom-call | tf_op jit(solution)/shard_map/pack/pallas_call | solution.py:312
  3.4 0.0 copy-start.4
  3.4 11.5 %all-to-all-start = ((bf16[128,8,128]{2,1,0:T(8,128)(2,1)}), bf16[128,8,128]{2,1,0:T(8,128)(2,1)S(1)}, u32[]{:S(2)}, u32[]{:S(2)}) async-start(bf16[128,8,128]{2,1,0:T(8,128)(2,1)} %bitcast.3), calls=%async_computation | async-start | bytes 524288 | tf_op jit(solution)/shard_map/all_to_all | solution.py:296
  14.9 0.0 copy-done.4
  15.0 0.1 slice.17
  15.0 0.0 copy-start.5
  15.0 0.7 copy-done.5
  15.7 0.1 slice.19
  15.8 0.0 copy-start.6
  15.9 0.6 copy-done.6
  16.5 0.6 reduce_sum.9
  17.1 0.1 rev.6
  17.2 0.1 rev.7
  17.3 0.1 pad.6.clone
  17.3 0.1 pad_add_fusion.place_ref
  17.4 8.3 %all-to-all-done = bf16[128,8,128]{2,1,0:T(8,128)(2,1)S(1)} async-done(((bf16[128,8,128]{2,1,0:T(8,128)(2,1)}), bf16[128,8,128]{2,1,0:T(8,128)(2,1)S(1)}, u32[]{:S(2)}, u32[]{:S(2)}) %all-to-all-start) | async-done | bytes 262176 | tf_op jit(solution)/shard_map/all_to_all | solution.py:296
  25.7 0.7 copy-done.2
  26.4 2.1 %pick.1 = (bf16[1536,128]{1,0:T(8,128)(2,1)}, f32[128,128]{1,0:T(8,128)S(1)}, f32[128,128]{1,0:T(8,128)S(1)}) custom-call(s32[2]{0:T(128)S(1)} %pad_add_fusion.place_ref, bf16[1024,128]{1,0:T(8,128)(2,1)S(1)} %bitcast.21, s32[1,128]{1,0:T(1,128)S(1)} %bitcast.24), custom_call_target="tpu_custom_call" | custom-call | tf_op jit(solution)/shard_map/pick/pallas_call | solution.py:321
  28.5 4.8 %all-to-all-start.1 = ((bf16[32,48,128]{2,1,0:T(8,128)(2,1)}), bf16[32,48,128]{2,1,0:T(8,128)(2,1)S(1)}, u32[]{:S(2)}, u32[]{:S(2)}) async-start(bf16[32,48,128]{2,1,0:T(8,128)(2,1)} %bitcast.6), calls=%async_computation.1 | async-start | bytes 786432 | tf_op jit(solution)/shard_map/all_to_all | solution.py:296
  33.3 0.7 broadcast_divide_fusion.weights_ref
  33.9 0.1 pad_maximum_fusion.1
  34.0 9.4 %all-to-all-done.1 = bf16[32,48,128]{2,1,0:T(8,128)(2,1)S(1)} async-done(((bf16[32,48,128]{2,1,0:T(8,128)(2,1)}), bf16[32,48,128]{2,1,0:T(8,128)(2,1)S(1)}, u32[]{:S(2)}, u32[]{:S(2)}) %all-to-all-start.1) | async-done | bytes 393248 | tf_op jit(solution)/shard_map/all_to_all | solution.py:296
  43.4 0.0 copy-done
  43.4 18.9 %litho.1 = bf16[2048,128]{1,0:T(8,128)(2,1)S(1)} custom-call(f32[12]{0:T(128)S(1)} %broadcast_divide_fusion.weights_ref, bf16[1536,128]{1,0:T(8,128)(2,1)S(1)} %bitcast.19, f32[256,384]{1,0:T(8,128)S(1)} %copy-done, f32[48,256]{1,0:T(8,128)S(1)} %concatenate.12.row_ref, f32[48,256]{1,0:T(8,128)S(1)} %get-tuple-element.13.row_rev_ref, ...), custom_call_target="tpu_custom_call" | custom-call | tf_op jit(solution)/shard_map/litho/pallas_call | solution.py:334
  62.3 17.1 %all_to_all.20 = bf16[128,16,128]{2,1,0:T(8,128)(2,1)S(1)} all-to-all(bf16[128,16,128]{2,1,0:T(8,128)(2,1)S(1)} %bitcast.17), channel_id=1, replica_groups=mesh['row'=4,'col'=32] {'row','col'}, dimensions={0} | all-to-all | bytes 1048576 | tf_op jit(solution)/shard_map/all_to_all | solution.py:296
  79.4 0.8 update.1
  80.1 15.5 %all_to_all.21 = bf16[128,8,128]{2,1,0:T(8,128)(2,1)S(1)} all-to-all(bf16[128,8,128]{2,1,0:T(8,128)(2,1)S(1)} %bitcast.20), channel_id=1, replica_groups=mesh['row'=4,'col'=32] {'row','col'}, dimensions={0} | all-to-all | bytes 524288 | tf_op jit(solution)/shard_map/all_to_all | solution.py:296
  95.6 0.9 unpack.1
  (7 shorter events, 0.0 us)
Async XLA Ops:
  0.6 0.7 copy-start.3
  1.3 0.8 copy-start.1
  3.4 11.5 %copy-start.4 = (bf16[24,2,35]{2,1,0:T(2,128)(2,1)S(1)}, bf16[24,2,35]{2,1,0:T(2,128)(2,1)}, u32[]{:S(2)}) copy-start(bf16[24,2,35]{2,1,0:T(2,128)(2,1)} %param.9) | copy-start | bytes 10084
  3.4 22.3 %all-to-all-start = ((bf16[128,8,128]{2,1,0:T(8,128)(2,1)}), bf16[128,8,128]{2,1,0:T(8,128)(2,1)S(1)}, u32[]{:S(2)}, u32[]{:S(2)}) async-start(bf16[128,8,128]{2,1,0:T(8,128)(2,1)} %bitcast.3), calls=%async_computation | async-start | bytes 524288 | tf_op jit(solution)/shard_map/all_to_all | solution.py:296
  15.0 0.7 copy-start.5
  15.8 0.7 copy-start.6
  25.7 0.7 copy-start.2
  28.5 15.0 %copy-start = (f32[256,384]{1,0:T(8,128)S(1)}, f32[256,384]{1,0:T(8,128)}, u32[]{:S(2)}) copy-start(f32[256,384]{1,0:T(8,128)} %target_ref.1) | copy-start | bytes 1179652
  28.5 14.9 %all-to-all-start.1 = ((bf16[32,48,128]{2,1,0:T(8,128)(2,1)}), bf16[32,48,128]{2,1,0:T(8,128)(2,1)S(1)}, u32[]{:S(2)}, u32[]{:S(2)}) async-start(bf16[32,48,128]{2,1,0:T(8,128)(2,1)} %bitcast.6), calls=%async_computation.1 | async-start | bytes 786432 | tf_op jit(solution)/shard_map/all_to_all | solution.py:296

commit v4 on v3

--- a/solution.py
+++ b/solution.py
@@ -58,26 +58,45 @@
     return jnp.broadcast_to(slots[:, s : s + 1], (slots.shape[0], BLK))
 
 
-def pack_kernel(blocks_ref, cells_ref, out_ref, stage):
+def pack_kernel(blocks_hbm, cells_hbm, out_hbm, blocks_ref, cells, stage, packed, ids_sem, in_sem, out_sem):
+    fetch_ids = pltpu.make_async_copy(blocks_hbm, blocks_ref, ids_sem)
+    fetch_ids.start()
+    fetch = pltpu.make_async_copy(cells_hbm, cells, in_sem)
+    fetch.start()
     lane = iota(1, (COLS, BLK))
     ids = jnp.full((COLS, BLK), -1.0, F32)
+    for s in range(ROWS + 1, 8):
+        stage[pl.ds(s, COLS, stride=8), :] = jnp.zeros((COLS, BLK), F32)
+    fetch_ids.wait()
     for n in range(6):
         ids = jnp.where(lane == n, blocks_ref[n // 3, n % 3].astype(F32), ids)
+    stage[pl.ds(ROWS, COLS, stride=8), :] = ids
+    fetch.wait()
     for s in range(ROWS):
-        stage[pl.ds(s, COLS, stride=8), :] = cells_ref[pl.ds(s, COLS, stride=ROWS), :]
-    stage[pl.ds(ROWS, COLS, stride=8), :] = ids
-    for s in range(ROWS + 1, 8):
-        stage[pl.ds(s, COLS, stride=8), :] = jnp.zeros((COLS, BLK), F32)
-    packed = stage[...].astype(BF)
-    for r in range(ROWS):
-        out_ref[r * COLS * 8 : (r + 1) * COLS * 8, :] = packed
-
-
-def pick_kernel(place_ref, first_ref, owner_ref, out_ref, held_ref, slots_ref, stage, mine, out_stage):
+        stage[pl.ds(s, COLS, stride=8), :] = cells[pl.ds(s, COLS, stride=ROWS), :]
+    packed[...] = stage[...].astype(BF)
+    copies = [
+        pltpu.make_async_copy(packed, out_hbm.at[pl.ds(r * COLS * 8, COLS * 8)], out_sem.at[r])
+        for r in range(ROWS)
+    ]
+    for copy in copies:
+        copy.start()
+    for copy in copies:
+        copy.wait()
+
+
+def pick_kernel(
+    place_ref, first_ref, owner_hbm, out_ref, held_ref, slots_ref, by_owner_ref,
+    owner_ref, stage, mine, out_stage, sem,
+):
+    fetch = pltpu.make_async_copy(owner_hbm, owner_ref, sem)
+    fetch.start()
     stage[...] = first_ref[...].astype(F32)
     slots = slot_ids(stage[pl.ds(ROWS, DEV, stride=8), :], place_ref[1])
     slots_ref[...] = slots
     table = jnp.concatenate([stage[pl.ds(s, DEV, stride=8), :] for s in range(ROWS)], 1)
+    fetch.wait()
+    by_owner_ref[...] = owner_select(owner_ref, True)
     held = dot(owner_select(owner_ref, False), table.astype(BF)).astype(BF)
     row = place_ref[0]
     own = held[:, :BLK].astype(F32)
@@ -154,14 +173,11 @@
 
     make_columns(0, columns_a)
 
-    def forward(i, carry):
-        make_columns(2 * i + 1, columns_b)
-        make_field(2 * i, columns_a)
-        make_columns(jnp.minimum(2 * i + 2, CHAN - 1), columns_a)
-        make_field(2 * i + 1, columns_b)
-        return carry
-
-    lax.fori_loop(0, CHAN // 2, forward, 0)
+    buffers = (columns_a, columns_b)
+    for k in range(CHAN):
+        if k + 1 < CHAN:
+            make_columns(k + 1, buffers[(k + 1) % 2])
+        make_field(k, buffers[k % 2])
     resist = jax.nn.sigmoid(3.0 * (light[...] - 1.3))
     light[...] = 2.0 * (resist - target_ref[...]) * 3.0 * resist * (1.0 - resist)
     grad[...] = jnp.zeros_like(grad)
@@ -203,21 +219,14 @@
                 back[:, 4 * q * BLK : 4 * (q + 1) * BLK], col_matrix
             )
 
-    make_back(0, 0, back_a)
-    make_back(1, 1, back_a)
-
-    def backward(i, carry):
-        k = 4 * i
-        make_back(k + 2, 0, back_b)
-        make_back(k + 3, 1, back_b)
-        add_grad(k, back_a)
-        later = jnp.minimum(k + 4, CHAN - 2)
-        make_back(later, 0, back_a)
-        make_back(later + 1, 1, back_a)
-        add_grad(k + 2, back_b)
-        return carry
-
-    lax.fori_loop(0, CHAN // 4, backward, 0)
+    backs = (back_a, back_b)
+    for j in range(2):
+        make_back(j, j, back_a)
+    for n in range(CHAN // 2):
+        if n + 1 < CHAN // 2:
+            for j in range(2):
+                make_back(2 * n + 2 + j, j, backs[(n + 1) % 2])
+        add_grad(2 * n, backs[n % 2])
     whole = pltpu.roll(pltpu.roll(grad[...], 384 - HALF, 0), 512 - HALF, 1)
     for q in range(4):
         wide[q] = whole[:, q * BLK : (q + 1) * BLK]
@@ -232,7 +241,7 @@
     out_ref[...] = stage[...].astype(BF)
 
 
-def update_kernel(recv_ref, slots_ref, owner_ref, held_ref, out_ref, stage, out_stage):
+def update_kernel(recv_ref, slots_ref, by_owner_ref, held_ref, out_ref, stage, out_stage):
     lane = iota(1)
     slots = slots_ref[...]
     slots_t = slots.T
@@ -257,8 +266,7 @@
         for q in range(3):
             select = (columns_of(slots, 4 * p + q) == cell).astype(BF)
             out_stage[pl.ds(3 * p + q, DEV, stride=8), :] = dot(select, updated)
-    by_owner = owner_select(owner_ref, True)
-    out_stage[pl.ds(6, DEV, stride=8), :] = dot(by_owner, total.astype(BF))
+    out_stage[pl.ds(6, DEV, stride=8), :] = dot(by_owner_ref[...], total.astype(BF))
     out_stage[pl.ds(7, DEV, stride=8), :] = jnp.zeros((DEV, BLK), F32)
     out_ref[...] = out_stage[...].astype(BF)
 
@@ -278,18 +286,23 @@
 
 SMEM = pl.BlockSpec(memory_space=pltpu.SMEM)
 VMEM = pl.BlockSpec(memory_space=pltpu.VMEM)
-
-
-def call(kernel, out_shape, in_specs, scratch, name, limit=8):
+HBM = pl.BlockSpec(memory_space=pltpu.HBM)
+
+
+def call(kernel, out_shape, in_specs, scratch, name, limit=8, out_space=VMEM):
     return pl.pallas_call(
         kernel,
         out_shape=out_shape,
         in_specs=in_specs,
-        out_specs=jax.tree.map(lambda _: VMEM, out_shape),
+        out_specs=jax.tree.map(lambda _: out_space, out_shape),
         scratch_shapes=scratch,
         name=name,
         compiler_params=pltpu.CompilerParams(vmem_limit_bytes=limit << 20),
     )
+
+
+def in_hbm(x):
+    return pltpu.with_memory_space_constraint(x, pltpu.HBM)
 
 
 def exchange(x, axes=AXES):
@@ -312,23 +325,34 @@
     first = call(
         pack_kernel,
         struct((DEV * 8, BLK), BF),
-        [SMEM, VMEM],
-        [pltpu.VMEM((COLS * 8, BLK), F32)],
+        [HBM, HBM],
+        [
+            pltpu.SMEM((2, 3), jnp.int32),
+            pltpu.VMEM((BLK, BLK), F32),
+            pltpu.VMEM((COLS * 8, BLK), F32),
+            pltpu.VMEM((COLS * 8, BLK), BF),
+            pltpu.SemaphoreType.DMA,
+            pltpu.SemaphoreType.DMA,
+            pltpu.SemaphoreType.DMA((ROWS,)),
+        ],
         "pack",
-    )(cell_of_block, cells.reshape(BLK, BLK))
+        out_space=HBM,
+    )(in_hbm(cell_of_block), in_hbm(cells.reshape(BLK, BLK)))
     first = exchange(first.reshape(DEV, 8, BLK)).reshape(DEV * 8, BLK)
 
-    picked, held, slots = call(
+    picked, held, slots, by_owner = call(
         pick_kernel,
-        (struct((COLS * PER_COL, BLK), BF), struct((BLK, BLK), F32), struct((DEV, BLK), F32)),
-        [SMEM, VMEM, VMEM],
+        (struct((COLS * PER_COL, BLK), BF), struct((BLK, BLK), F32), struct((DEV, BLK), F32), struct((DEV, DEV), BF)),
+        [SMEM, VMEM, HBM],
         [
+            pltpu.VMEM((1, DEV), jnp.int32),
             pltpu.VMEM((DEV * 8, BLK), F32),
             pltpu.VMEM((COLS, BLK), F32),
             pltpu.VMEM((COLS * PER_COL, BLK), F32),
+            pltpu.SemaphoreType.DMA,
         ],
         "pick",
-    )(place, first, owner)
+    )(place, first, in_hbm(owner))
     received = exchange(picked.reshape(COLS, PER_COL, BLK), "col").reshape(COLS * PER_COL, BLK)
 
     pieces = call(
@@ -362,7 +386,7 @@
         [VMEM] * 4,
         [pltpu.VMEM((DEV * SLOTS, BLK), F32), pltpu.VMEM((DEV * 8, BLK), F32)],
         "update",
-    )(pieces, slots, owner, held)
+    )(pieces, slots, by_owner, held)
     results = exchange(results.reshape(DEV, 8, BLK)).reshape(DEV * 8, BLK)
 
     gradient, new_mask = call(

time: 97 us -> 91.3 us (0.941)
  Pallas kernels: 23.9 us -> 20.4 us
  local copies, waits for them, and re-layouts: 3.92 us -> 1.76 us
    pallas_call x1, Pallas kernels: 18.9 us -> 14.5 us  [per_device(): call(litho_kernel, struct((DEV * SLOTS, BLK), BF), [SMEM] + [VMEM] * 6, [...]
    unnamed x14 -> x8, local copies, waits for them, and re-layouts: 3.53 us -> 1.37 us
where the time goes in v4:
time: 91.3 us; the launch traced here: 90.8 us
  blocking collectives  32.5 us (36%)
  Pallas kernels  20.4 us (22%)
  waiting for transfers between devices  17.7 us (19%)
  starting transfers between devices  16.3 us (18%)
  local copies, waits for them, and re-layouts  1.76 us (2%)
  other arithmetic  1.41 us (2%)
    all_to_all x2, blocking collectives, exchange(): return lax.all_to_all(x, axes, 0, 0, tiled=True)  32.5 us
    all_to_all x2, waiting for transfers between devices, exchange(): return lax.all_to_all(x, axes, 0, 0, tiled=True)  17.7 us
    all_to_all x2, starting transfers between devices, exchange(): return lax.all_to_all(x, axes, 0, 0, tiled=True)  16.3 us
    pallas_call x1, Pallas kernels, per_device(): call(litho_kernel, struct((DEV * SLOTS, BLK), BF), [SMEM] + [VMEM] * 6, [...  14.5 us
    pallas_call x1, Pallas kernels, per_device(): call(pick_kernel, (struct((COLS * PER_COL, BLK), BF), struct((BLK, BLK),...  2.61 us
  transfers between devices with their start and end apart: 2, of which 2 were waited for; matrix products, arithmetic and copies ran while one was open for 2% of the time, Pallas kernels for 0%

profile of v4, /device:TPU:1, one launch (start us, length us, event | category | flops | bytes accessed | tf_op | source)
XLA Modules:
  0.0 90.8 jit_solution(6212074253975603820)
XLA Ops:
  0.6 1.6 %pack.1 = bf16[1024,128]{1,0:T(8,128)(2,1)} custom-call(s32[2,3]{1,0:T(2,128)} %blocks_hbm.1, f32[128,128]{1,0:T(8,128)} %bitcast.29), custom_call_target="tpu_custom_call" | custom-call | tf_op jit(solution)/shard_map/pack/pallas_call | solution.py:325
  2.3 0.0 copy-start.1
  2.3 11.5 %all-to-all-start = ((bf16[128,8,128]{2,1,0:T(8,128)(2,1)}), bf16[128,8,128]{2,1,0:T(8,128)(2,1)S(1)}, u32[]{:S(2)}, u32[]{:S(2)}) async-start(bf16[128,8,128]{2,1,0:T(8,128)(2,1)} %bitcast.3), calls=%async_computation | async-start | bytes 524288 | tf_op jit(solution)/shard_map/all_to_all | solution.py:309
  13.8 0.0 copy-done.1
  13.8 0.1 slice.17
  13.9 0.0 copy-start.2
  13.9 0.7 copy-done.2
  14.6 0.1 slice.19
  14.7 0.0 copy-start.3
  14.7 0.6 copy-done.3
  15.3 0.6 reduce_sum.9
  15.9 0.1 rev.6
  16.0 0.1 rev.7
  16.1 0.1 pad.6.clone
  16.2 0.1 pad_add_fusion.place_ref
  16.2 8.3 %all-to-all-done = bf16[128,8,128]{2,1,0:T(8,128)(2,1)S(1)} async-done(((bf16[128,8,128]{2,1,0:T(8,128)(2,1)}), bf16[128,8,128]{2,1,0:T(8,128)(2,1)S(1)}, u32[]{:S(2)}, u32[]{:S(2)}) %all-to-all-start) | async-done | bytes 262176 | tf_op jit(solution)/shard_map/all_to_all | solution.py:309
  24.6 2.6 %pick.1 = (bf16[1536,128]{1,0:T(8,128)(2,1)}, f32[128,128]{1,0:T(8,128)S(1)}, f32[128,128]{1,0:T(8,128)S(1)}, bf16[128,128]{1,0:T(8,128)(2,1)S(1)}) custom-call(s32[2]{0:T(128)S(1)} %pad_add_fusion.place_ref, bf16[1024,128]{1,0:T(8,128)(2,1)S(1)} %bitcast.20, s32[1,128]{1,0:T(1,128)} %bitcast.30), custom_call_target="tpu_custom_call" | custom-call | tf_op jit(solution)/shard_map/pick/pallas_call | solution.py:343
  27.2 0.0 copy-start
  27.2 4.8 %all-to-all-start.1 = ((bf16[32,48,128]{2,1,0:T(8,128)(2,1)}), bf16[32,48,128]{2,1,0:T(8,128)(2,1)S(1)}, u32[]{:S(2)}, u32[]{:S(2)}) async-start(bf16[32,48,128]{2,1,0:T(8,128)(2,1)} %bitcast.6), calls=%async_computation.1 | async-start | bytes 786432 | tf_op jit(solution)/shard_map/all_to_all | solution.py:309
  32.0 0.7 broadcast_divide_fusion.weights_ref
  32.7 0.1 pad_maximum_fusion.1
  32.8 9.4 %all-to-all-done.1 = bf16[32,48,128]{2,1,0:T(8,128)(2,1)S(1)} async-done(((bf16[32,48,128]{2,1,0:T(8,128)(2,1)}), bf16[32,48,128]{2,1,0:T(8,128)(2,1)S(1)}, u32[]{:S(2)}, u32[]{:S(2)}) %all-to-all-start.1) | async-done | bytes 393248 | tf_op jit(solution)/shard_map/all_to_all | solution.py:309
  42.2 0.0 copy-done
  42.2 14.5 %litho.1 = bf16[2048,128]{1,0:T(8,128)(2,1)S(1)} custom-call(f32[12]{0:T(128)S(1)} %broadcast_divide_fusion.weights_ref, bf16[1536,128]{1,0:T(8,128)(2,1)S(1)} %bitcast.19, f32[256,384]{1,0:T(8,128)S(1)} %copy-done, f32[48,256]{1,0:T(8,128)S(1)} %concatenate.12.row_ref, f32[48,256]{1,0:T(8,128)S(1)} %get-tuple-element.15.row_rev_ref, ...), custom_call_target="tpu_custom_call" | custom-call | tf_op jit(solution)/shard_map/litho/pallas_call | solution.py:358
  56.7 17.0 %all_to_all.20 = bf16[128,16,128]{2,1,0:T(8,128)(2,1)S(1)} all-to-all(bf16[128,16,128]{2,1,0:T(8,128)(2,1)S(1)} %bitcast.17), channel_id=1, replica_groups=mesh['row'=4,'col'=32] {'row','col'}, dimensions={0} | all-to-all | bytes 1048576 | tf_op jit(solution)/shard_map/all_to_all | solution.py:309
  73.7 0.7 update.1
  74.5 15.5 %all_to_all.21 = bf16[128,8,128]{2,1,0:T(8,128)(2,1)S(1)} all-to-all(bf16[128,8,128]{2,1,0:T(8,128)(2,1)S(1)} %bitcast.22), channel_id=1, replica_groups=mesh['row'=4,'col'=32] {'row','col'}, dimensions={0} | all-to-all | bytes 524288 | tf_op jit(solution)/shard_map/all_to_all | solution.py:309
  89.9 0.9 unpack.1
  (5 shorter events, 0.0 us)
Async XLA Ops:
  2.3 11.5 %copy-start.1 = (bf16[24,2,35]{2,1,0:T(2,128)(2,1)S(1)}, bf16[24,2,35]{2,1,0:T(2,128)(2,1)}, u32[]{:S(2)}) copy-start(bf16[24,2,35]{2,1,0:T(2,128)(2,1)} %param.9) | copy-start | bytes 10084
  2.3 22.3 %all-to-all-start = ((bf16[128,8,128]{2,1,0:T(8,128)(2,1)}), bf16[128,8,128]{2,1,0:T(8,128)(2,1)S(1)}, u32[]{:S(2)}, u32[]{:S(2)}) async-start(bf16[128,8,128]{2,1,0:T(8,128)(2,1)} %bitcast.3), calls=%async_computation | async-start | bytes 524288 | tf_op jit(solution)/shard_map/all_to_all | solution.py:309
  13.9 0.7 copy-start.2
  14.7 0.7 copy-start.3
  27.2 15.0 %copy-start = (f32[256,384]{1,0:T(8,128)S(1)}, f32[256,384]{1,0:T(8,128)}, u32[]{:S(2)}) copy-start(f32[256,384]{1,0:T(8,128)} %target_ref.1) | copy-start | bytes 1179652
  27.2 15.0 %all-to-all-start.1 = ((bf16[32,48,128]{2,1,0:T(8,128)(2,1)}), bf16[32,48,128]{2,1,0:T(8,128)(2,1)S(1)}, u32[]{:S(2)}, u32[]{:S(2)}) async-start(bf16[32,48,128]{2,1,0:T(8,128)(2,1)} %bitcast.6), calls=%async_computation.1 | async-start | bytes 786432 | tf_op jit(solution)/shard_map/all_to_all | solution.py:309

commit v5 on v4

--- a/solution.py
+++ b/solution.py
@@ -5,17 +5,18 @@
 from jax.experimental.pallas import tpu as pltpu
 from jax.sharding import PartitionSpec as P
 
+
 AXES = ("row", "col")
 ROWS, COLS = 4, 32
 DEV = ROWS * COLS
 BLK = 128
 HALF = 17
-WIN = BLK + 2 * HALF
 TILE_R, TILE_C = 256, 384
-EXT_R = 296
-TAIL = 48
+COL_R = TILE_R + 72
+FIELD_R = 304
+SPLIT = 144
 CHAN = 24
-SLOTS = 16
+SLOTS = 8
 PER_COL = 12 * ROWS
 BF, F32 = jnp.bfloat16, jnp.float32
 
@@ -119,16 +120,16 @@
     out_ref[...] = out_stage[...].astype(BF)
 
 
-def toeplitz(taps_ref, m):
-    base = jnp.broadcast_to(taps_ref[pl.ds(m, 1), :], (BLK, 2 * BLK))
+def toeplitz(taps_ref, m, rows=BLK):
+    base = jnp.broadcast_to(taps_ref[pl.ds(m, 1), :], (rows, 2 * BLK))
     return pltpu.roll(base, 0, 1, stride=1, stride_axis=0).astype(BF)
 
 
 def litho_kernel(
-    weights_ref, recv_ref, target_ref, row_ref, row_rev_ref, col_ref, col_rev_ref,
+    place_ref, weights_ref, recv_ref, target_ref, row_ref, row_flip_ref, col_ref, col_rev_ref,
     out_ref, stage, wide, mask, columns_a, columns_b, field, light, grad, back_a, back_b,
 ):
-    stage[: COLS * PER_COL, :] = recv_ref[...].astype(F32)
+    stage[...] = recv_ref[...].astype(F32)
     for q in range(4):
         for p in range(3):
             for s in range(ROWS):
@@ -136,9 +137,9 @@
                     pl.ds(ROWS * (4 * p + q) + s, COLS, stride=PER_COL), :
                 ]
     whole = jnp.concatenate([wide[q] for q in range(4)], 1)
-    mask[...] = pltpu.roll(pltpu.roll(whole, HALF, 1), HALF, 0)[:EXT_R].astype(BF)
+    mask[...] = pltpu.roll(pltpu.roll(whole, HALF, 1), 2 * HALF, 0)[:COL_R].astype(BF)
     for columns in (columns_a, columns_b):
-        columns[:, EXT_R:, :] = jnp.zeros((2, 384 - EXT_R, TILE_C), BF)
+        columns[:, COL_R:, :] = jnp.zeros((2, SPLIT + 2 * BLK - COL_R, TILE_C), BF)
     light[...] = jnp.zeros_like(light)
 
     def make_columns(k, columns):
@@ -153,13 +154,13 @@
         for q in range(3):
             made = dot(mask[:, q * BLK : (q + 2) * BLK], col_matrix).astype(BF)
             for r in range(2):
-                columns[r, :EXT_R, q * BLK : (q + 1) * BLK] = made[:, r * BLK : (r + 1) * BLK]
+                columns[r, :COL_R, q * BLK : (q + 1) * BLK] = made[:, r * BLK : (r + 1) * BLK]
 
     def make_field(k, columns):
-        row_matrix = jnp.concatenate([toeplitz(row_ref, 2 * k + r) for r in range(2)], 1)
+        row_matrix = jnp.concatenate([toeplitz(row_ref, 2 * k + r, FIELD_R - SPLIT) for r in range(2)], 1)
         weight = weights_ref[k // 2]
         windows = [
-            jnp.concatenate([columns[r, p * BLK : (p + 2) * BLK, :] for r in range(2)], 0)
+            jnp.concatenate([columns[r, p * SPLIT : p * SPLIT + 2 * BLK, :] for r in range(2)], 0)
             for p in range(2)
         ]
         last = dot(row_matrix, jnp.concatenate([w[:, 2 * BLK :] for w in windows], 1))
@@ -167,7 +168,8 @@
             made = jnp.concatenate(
                 [dot(row_matrix, windows[p][:, : 2 * BLK]), last[:, p * BLK : (p + 1) * BLK]], 1
             )
-            here = slice(p * BLK, (p + 1) * BLK)
+            here = slice(p * SPLIT, FIELD_R if p else SPLIT)
+            made = made[: here.stop - here.start]
             light[here] += weight * made * made
             field[k, here] = made
 
@@ -179,26 +181,22 @@
             make_columns(k + 1, buffers[(k + 1) % 2])
         make_field(k, buffers[k % 2])
     resist = jax.nn.sigmoid(3.0 * (light[...] - 1.3))
-    light[...] = 2.0 * (resist - target_ref[...]) * 3.0 * resist * (1.0 - resist)
+    error = 2.0 * (resist - target_ref[...]) * 3.0 * resist * (1.0 - resist)
+    at_row = iota(0, (FIELD_R, TILE_C))
+    first = jnp.where(place_ref[0] == 0, HALF, 0)
+    end = jnp.where(place_ref[0] == ROWS - 1, HALF + TILE_R, FIELD_R)
+    light[...] = jnp.where((at_row >= first) & (at_row < end), error, 0.0)
     grad[...] = jnp.zeros_like(grad)
 
     def make_back(k, j, back):
-        weight = 2.0 * weights_ref[k // 2]
-        upper, lower = [
-            (weight * field[k, p * BLK : (p + 1) * BLK] * light[p * BLK : (p + 1) * BLK]).astype(BF)
-            for p in range(2)
+        weighted = (2.0 * weights_ref[k // 2] * field[k] * light[...]).astype(BF)
+        taps = jnp.concatenate([toeplitz(row_flip_ref, 2 * k + r) for r in range(2)], 0)
+        windows = [
+            weighted[: 2 * BLK],
+            jnp.concatenate([weighted[BLK:], jnp.zeros((3 * BLK - FIELD_R, TILE_C), BF)], 0),
         ]
-        rolled = [toeplitz(row_rev_ref, 2 * k + r) for r in range(2)]
-        both = jnp.concatenate(rolled, 0)
-        tail = jnp.concatenate([t[:TAIL, BLK:] for t in rolled], 0)
-        second = jnp.concatenate([lower, upper], 0)
-        first = jnp.concatenate([upper, jnp.zeros_like(upper)], 0)
-        last = dot(both, jnp.concatenate([first[:, 2 * BLK :], second[:, 2 * BLK :]], 1)).astype(BF)
-        parts = [
-            dot(both[:, :BLK], upper[:, : 2 * BLK]).astype(BF),
-            dot(both, second[:, : 2 * BLK]).astype(BF),
-        ]
-        end = dot(tail, lower).astype(BF)
+        last = dot(taps, jnp.concatenate([w[:, 2 * BLK :] for w in windows], 1)).astype(BF)
+        parts = [dot(taps, w[:, : 2 * BLK]).astype(BF) for w in windows]
         for r in range(2):
             for q in range(3):
                 at = (4 * q + 2 * j + r) * BLK
@@ -208,14 +206,11 @@
                     back[p * BLK : (p + 1) * BLK, at : at + BLK] = piece[
                         r * BLK : (r + 1) * BLK, lanes : lanes + BLK
                     ]
-                back[2 * BLK :, at : at + BLK] = end[
-                    r * TAIL : r * TAIL + EXT_R - 2 * BLK, q * BLK : (q + 1) * BLK
-                ]
 
     def add_grad(k, back):
         col_matrix = jnp.concatenate([toeplitz(col_ref, 2 * k + r) for r in range(4)], 0)
         for q in range(3):
-            grad[:EXT_R, q * BLK : (q + 2) * BLK] += dot(
+            grad[:, q * BLK : (q + 2) * BLK] += dot(
                 back[:, 4 * q * BLK : 4 * (q + 1) * BLK], col_matrix
             )
 
@@ -227,18 +222,16 @@
             for j in range(2):
                 make_back(2 * n + 2 + j, j, backs[(n + 1) % 2])
         add_grad(2 * n, backs[n % 2])
-    whole = pltpu.roll(pltpu.roll(grad[...], 384 - HALF, 0), 512 - HALF, 1)
+    whole = pltpu.roll(grad[...], 512 - HALF, 1)
     for q in range(4):
-        wide[q] = whole[:, q * BLK : (q + 1) * BLK]
+        wide[q, :TILE_R] = whole[:, q * BLK : (q + 1) * BLK]
     for q in range(4):
-        for p in range(3):
+        for p in range(2):
             for r in range(ROWS):
                 stage[pl.ds(r * COLS * SLOTS + 4 * p + q, COLS, stride=SLOTS), :] = wide[
                     q, pl.ds(p * BLK + r, COLS, stride=ROWS), :
                 ]
-    for s in range(12, SLOTS):
-        stage[pl.ds(s, DEV, stride=SLOTS), :] = jnp.zeros((DEV, BLK), F32)
-    out_ref[...] = stage[...].astype(BF)
+    out_ref[...] = stage[: DEV * SLOTS].astype(BF)
 
 
 def update_kernel(recv_ref, slots_ref, by_owner_ref, held_ref, out_ref, stage, out_stage):
@@ -254,7 +247,7 @@
 
     total = jnp.zeros((BLK, BLK), F32)
     from_left, from_right = total, total
-    for p in range(3):
+    for p in range(2):
         for q in range(3):
             total += gather(4 * p + q, 4 * p + q)
         from_left += gather(4 * p + 3, 4 * p + 3)
@@ -289,14 +282,13 @@
 HBM = pl.BlockSpec(memory_space=pltpu.HBM)
 
 
-def call(kernel, out_shape, in_specs, scratch, name, limit=8, out_space=VMEM):
+def call(kernel, out_shape, in_specs, scratch, limit=8, out_space=VMEM):
     return pl.pallas_call(
         kernel,
         out_shape=out_shape,
         in_specs=in_specs,
         out_specs=jax.tree.map(lambda _: out_space, out_shape),
         scratch_shapes=scratch,
-        name=name,
         compiler_params=pltpu.CompilerParams(vmem_limit_bytes=limit << 20),
     )
 
@@ -321,6 +313,20 @@
         if reverse:
             return jnp.concatenate([flat[:, :1], gap, flat[:, :0:-1]], 1)
         return jnp.concatenate([flat, gap], 1)
+
+    down = [(i, i + 1) for i in range(ROWS - 1)]
+    up = [(i + 1, i) for i in range(ROWS - 1)]
+    above = lax.ppermute(target[TILE_R - HALF :], "row", down)
+    below = lax.ppermute(target[:HALF], "row", up)
+    wide_target = jnp.concatenate(
+        [
+            above,
+            target,
+            below,
+            jnp.zeros((FIELD_R - TILE_R - 2 * HALF, TILE_C), F32),
+        ],
+        0,
+    )
 
     first = call(
         pack_kernel,
@@ -335,10 +341,10 @@
             pltpu.SemaphoreType.DMA,
             pltpu.SemaphoreType.DMA((ROWS,)),
         ],
-        "pack",
         out_space=HBM,
     )(in_hbm(cell_of_block), in_hbm(cells.reshape(BLK, BLK)))
-    first = exchange(first.reshape(DEV, 8, BLK)).reshape(DEV * 8, BLK)
+    first = exchange(first.reshape(DEV, 8, BLK))
+    first = first.reshape(DEV * 8, BLK)
 
     picked, held, slots, by_owner = call(
         pick_kernel,
@@ -351,31 +357,30 @@
             pltpu.VMEM((COLS * PER_COL, BLK), F32),
             pltpu.SemaphoreType.DMA,
         ],
-        "pick",
     )(place, first, in_hbm(owner))
-    received = exchange(picked.reshape(COLS, PER_COL, BLK), "col").reshape(COLS * PER_COL, BLK)
+    received = exchange(picked.reshape(COLS, PER_COL, BLK), "col")
+    received = received.reshape(COLS * PER_COL, BLK)
 
     pieces = call(
         litho_kernel,
         struct((DEV * SLOTS, BLK), BF),
-        [SMEM] + [VMEM] * 6,
+        [SMEM] * 2 + [VMEM] * 6,
         [
-            pltpu.VMEM((DEV * SLOTS, BLK), F32),
+            pltpu.VMEM((COLS * PER_COL, BLK), F32),
             pltpu.VMEM((4, 384, BLK), F32),
-            pltpu.VMEM((EXT_R, 512), BF),
-            pltpu.VMEM((2, 384, TILE_C), BF),
-            pltpu.VMEM((2, 384, TILE_C), BF),
-            pltpu.VMEM((CHAN, TILE_R, TILE_C), F32),
-            pltpu.VMEM((TILE_R, TILE_C), F32),
-            pltpu.VMEM((384, 512), F32),
-            pltpu.VMEM((EXT_R, 12 * BLK), BF),
-            pltpu.VMEM((EXT_R, 12 * BLK), BF),
+            pltpu.VMEM((COL_R, 512), BF),
+            pltpu.VMEM((2, SPLIT + 2 * BLK, TILE_C), BF),
+            pltpu.VMEM((2, SPLIT + 2 * BLK, TILE_C), BF),
+            pltpu.VMEM((CHAN, FIELD_R, TILE_C), F32),
+            pltpu.VMEM((FIELD_R, TILE_C), F32),
+            pltpu.VMEM((TILE_R, 512), F32),
+            pltpu.VMEM((TILE_R, 12 * BLK), BF),
+            pltpu.VMEM((TILE_R, 12 * BLK), BF),
         ],
-        "litho",
         32,
     )(
-        weights, received, target,
-        spread(row_taps, False), spread(row_taps, True),
+        place, weights, received, wide_target,
+        spread(row_taps, False), spread(row_taps[:, :, ::-1], False),
         spread(col_taps, False), spread(col_taps, True),
     )
     pieces = exchange(pieces.reshape(DEV, SLOTS, BLK)).reshape(DEV * SLOTS, BLK)
@@ -385,7 +390,6 @@
         struct((DEV * 8, BLK), BF),
         [VMEM] * 4,
         [pltpu.VMEM((DEV * SLOTS, BLK), F32), pltpu.VMEM((DEV * 8, BLK), F32)],
-        "update",
     )(pieces, slots, by_owner, held)
     results = exchange(results.reshape(DEV, 8, BLK)).reshape(DEV * 8, BLK)
 
@@ -394,7 +398,6 @@
         (struct((BLK, BLK), F32), struct((TILE_R, TILE_C), F32)),
         [VMEM],
         [pltpu.VMEM((DEV * 8, BLK), F32), pltpu.VMEM((3, TILE_R, BLK), F32)],
-        "unpack",
     )(results)
     return gradient.reshape(1, BLK, BLK), new_mask
 

time: 91.3 us -> 94.8 us (1.038)
  starting transfers between devices: 16.3 us -> 22.3 us
  blocking collectives: 32.5 us -> 29.8 us
    ppermute x0 -> x2, starting transfers between devices: none -> 5.22 us  [the longest x1 3.92 us: per_device(): above = lax.ppermute(target[TILE_R - HALF:], 'row', down)]
    all_to_all x2, blocking collectives: 32.5 us -> 29.8 us  [exchange(): return lax.all_to_all(x, axes, 0, 0, tiled=True)]
  transfers between devices with their start and end apart: 2 -> 4, of which waited for: 2 -> 2; matrix products, arithmetic and copies ran while one was open for 2% -> 2% of each run, Pallas kernels for 0% -> 4%
where the time goes in v5:
time: 94.8 us; the launch traced here: 94.3 us
  blocking collectives  29.8 us (31%)
  starting transfers between devices  22.3 us (24%)
  Pallas kernels  19.9 us (21%)
  waiting for transfers between devices  17.5 us (18%)
  local copies, waits for them, and re-layouts  2.45 us (3%)
  other arithmetic  1.52 us (2%)
    all_to_all x2, blocking collectives, exchange(): return lax.all_to_all(x, axes, 0, 0, tiled=True)  29.8 us
    all_to_all x2, waiting for transfers between devices, exchange(): return lax.all_to_all(x, axes, 0, 0, tiled=True)  17.5 us
    all_to_all x2, starting transfers between devices, exchange(): return lax.all_to_all(x, axes, 0, 0, tiled=True)  17.1 us
    pallas_call x1, Pallas kernels, per_device(): call(litho_kernel, struct((DEV * SLOTS, BLK), BF), [SMEM] * 2 + [VMEM] *...  14.2 us
    ppermute x1, starting transfers between devices, per_device(): above = lax.ppermute(target[TILE_R - HALF:], 'row', down)  3.92 us
    pallas_call x1, Pallas kernels, per_device(): call(pick_kernel, (struct((COLS * PER_COL, BLK), BF), struct((BLK, BLK),...  2.62 us
  transfers between devices with their start and end apart: 4, of which 2 were waited for; matrix products, arithmetic and copies ran while one was open for 2% of the time, Pallas kernels for 4%

profile of v5, /device:TPU:1, one launch (start us, length us, event | category | flops | bytes accessed | tf_op | source)
XLA Modules:
  0.0 94.3 jit_solution(4374120755539467631)
XLA Ops:
  0.6 0.8 fusion
  1.4 3.9 %collective-permute-start = (f32[17,384]{1,0:T(8,128)S(1)}, f32[17,384]{1,0:T(8,128)S(1)}, u32[]{:S(2)}, u32[]{:S(2)}) collective-permute-start(f32[17,384]{1,0:T(8,128)S(1)} %get-tuple-element.14), channel_id=1, source_target_pairs={{0,32},{32,64},{64,96},{1,33},{33,65},{65,97},{2,34},{34,66},{66,9... | collective-permute-start | bytes 78344 | tf_op jit(solution)/shard_map/ppermute | solution.py:319
  5.4 1.3 %collective-permute-start.1 = (f32[17,384]{1,0:T(8,128)S(1)}, f32[17,384]{1,0:T(8,128)S(1)}, u32[]{:S(2)}, u32[]{:S(2)}) collective-permute-start(f32[17,384]{1,0:T(8,128)S(1)} %get-tuple-element.15), channel_id=1, source_target_pairs={{32,0},{64,32},{96,64},{33,1},{65,33},{97,65},{34,2},{66,34},{98,6... | collective-permute-start | bytes 78344 | tf_op jit(solution)/shard_map/ppermute | solution.py:320
  6.7 1.6 %shard_map.86 = bf16[1024,128]{1,0:T(8,128)(2,1)} custom-call(s32[2,3]{1,0:T(2,128)} %blocks_hbm.1, f32[128,128]{1,0:T(8,128)} %bitcast.26), custom_call_target="tpu_custom_call" | custom-call | tf_op jit(solution)/shard_map/pallas_call | solution.py:331
  8.3 12.1 %all-to-all-start = ((bf16[128,8,128]{2,1,0:T(8,128)(2,1)}), bf16[128,8,128]{2,1,0:T(8,128)(2,1)S(1)}, u32[]{:S(2)}, u32[]{:S(2)}) async-start(bf16[128,8,128]{2,1,0:T(8,128)(2,1)} %bitcast.3), calls=%async_computation | async-start | bytes 524288 | tf_op jit(solution)/shard_map/all_to_all | solution.py:301
  20.4 0.0 copy-start.1
  20.4 0.1 pad_add_fusion.place_ref
  20.5 0.6 copy-done.1
  21.1 0.1 slice.17
  21.2 0.1 rev.7
  21.3 0.6 copy-done.3
  21.8 0.6 reduce_sum.9
  22.4 0.1 pad.6.clone
  22.5 0.1 pad_maximum_fusion.col_rev_ref
  22.6 8.6 %all-to-all-done = bf16[128,8,128]{2,1,0:T(8,128)(2,1)S(1)} async-done(((bf16[128,8,128]{2,1,0:T(8,128)(2,1)}), bf16[128,8,128]{2,1,0:T(8,128)(2,1)S(1)}, u32[]{:S(2)}, u32[]{:S(2)}) %all-to-all-start) | async-done | bytes 262176 | tf_op jit(solution)/shard_map/all_to_all | solution.py:301
  31.2 2.6 %shard_map.87 = (bf16[1536,128]{1,0:T(8,128)(2,1)}, f32[128,128]{1,0:T(8,128)S(1)}, f32[128,128]{1,0:T(8,128)S(1)}, bf16[128,128]{1,0:T(8,128)(2,1)S(1)}) custom-call(s32[2]{0:T(128)S(1)} %pad_add_fusion.place_ref, bf16[1024,128]{1,0:T(8,128)(2,1)S(1)} %bitcast.18, s32[1,128]{1,0:T(1,128)} %bitcast.29), custom_call_target="tpu_custom_call" | custom-call | tf_op jit(solution)/shard_map/pallas_call | solution.py:349
  33.8 0.0 copy-start.2
  33.8 0.0 copy-start
  33.8 5.0 %all-to-all-start.1 = ((bf16[32,48,128]{2,1,0:T(8,128)(2,1)}), bf16[32,48,128]{2,1,0:T(8,128)(2,1)S(1)}, u32[]{:S(2)}, u32[]{:S(2)}) async-start(bf16[32,48,128]{2,1,0:T(8,128)(2,1)} %bitcast.6), calls=%async_computation.1 | async-start | bytes 786432 | tf_op jit(solution)/shard_map/all_to_all | solution.py:301
  38.8 0.7 broadcast_divide_fusion.weights_ref
  39.5 0.0 copy-done.2
  39.5 0.1 rev.6
  39.7 0.1 pad.11.clone
  39.8 0.0 collective-permute-done
  39.8 0.0 collective-permute-done.1
  39.8 0.1 maximum_maximum_fusion.target_ref
  39.9 8.9 %all-to-all-done.1 = bf16[32,48,128]{2,1,0:T(8,128)(2,1)S(1)} async-done(((bf16[32,48,128]{2,1,0:T(8,128)(2,1)}), bf16[32,48,128]{2,1,0:T(8,128)(2,1)S(1)}, u32[]{:S(2)}, u32[]{:S(2)}) %all-to-all-start.1) | async-done | bytes 393248 | tf_op jit(solution)/shard_map/all_to_all | solution.py:301
  48.8 14.2 %shard_map.88 = bf16[1024,128]{1,0:T(8,128)(2,1)S(1)} custom-call(s32[2]{0:T(128)S(1)} %pad_add_fusion.place_ref, f32[12]{0:T(128)S(1)} %broadcast_divide_fusion.weights_ref, bf16[1536,128]{1,0:T(8,128)(2,1)S(1)} %bitcast.17, f32[304,384]{1,0:T(8,128)S(1)} %maximum_maximum_fusion.target_ref, f32[48,256]{1,0:T(8,128)S(1)} %get-tuple-element.17.row_ref, ...), custom_call_target="tpu_custom_call" | custom-call | tf_op jit(solution)/shard_map/pallas_call | solution.py:364
  63.0 14.4 %all_to_all.20 = bf16[128,8,128]{2,1,0:T(8,128)(2,1)S(1)} all-to-all(bf16[128,8,128]{2,1,0:T(8,128)(2,1)S(1)} %bitcast.22), channel_id=1, replica_groups=mesh['row'=4,'col'=32] {'row','col'}, dimensions={0} | all-to-all | bytes 524288 | tf_op jit(solution)/shard_map/all_to_all | solution.py:301
  77.5 0.6 shard_map.89
  78.1 15.3 %all_to_all.21 = bf16[128,8,128]{2,1,0:T(8,128)(2,1)S(1)} all-to-all(bf16[128,8,128]{2,1,0:T(8,128)(2,1)S(1)} %bitcast.20), channel_id=1, replica_groups=mesh['row'=4,'col'=32] {'row','col'}, dimensions={0} | all-to-all | bytes 524288 | tf_op jit(solution)/shard_map/all_to_all | solution.py:301
  93.4 0.9 shard_map.90
  (7 shorter events, 0.0 us)
Async XLA Ops:
  1.4 38.3 %collective-permute-start = (f32[17,384]{1,0:T(8,128)S(1)}, f32[17,384]{1,0:T(8,128)S(1)}, u32[]{:S(2)}, u32[]{:S(2)}) collective-permute-start(f32[17,384]{1,0:T(8,128)S(1)} %get-tuple-element.14), channel_id=1, source_target_pairs={{0,32},{32,64},{64,96},{1,33},{33,65},{65,97},{2,34},{34,66},{66,9... | collective-permute-start | bytes 78344 | tf_op jit(solution)/shard_map/ppermute | solution.py:319
  5.4 34.4 %collective-permute-start.1 = (f32[17,384]{1,0:T(8,128)S(1)}, f32[17,384]{1,0:T(8,128)S(1)}, u32[]{:S(2)}, u32[]{:S(2)}) collective-permute-start(f32[17,384]{1,0:T(8,128)S(1)} %get-tuple-element.15), channel_id=1, source_target_pairs={{32,0},{64,32},{96,64},{33,1},{65,33},{97,65},{34,2},{66,34},{98,6... | collective-permute-start | bytes 78344 | tf_op jit(solution)/shard_map/ppermute | solution.py:320
  8.3 22.9 %all-to-all-start = ((bf16[128,8,128]{2,1,0:T(8,128)(2,1)}), bf16[128,8,128]{2,1,0:T(8,128)(2,1)S(1)}, u32[]{:S(2)}, u32[]{:S(2)}) async-start(bf16[128,8,128]{2,1,0:T(8,128)(2,1)} %bitcast.3), calls=%async_computation | async-start | bytes 524288 | tf_op jit(solution)/shard_map/all_to_all | solution.py:301
  20.4 0.7 copy-start.1
  21.2 0.7 copy-start.3
  33.8 5.7 %copy-start.2 = (bf16[24,2,35]{2,1,0:T(2,128)(2,1)S(1)}, bf16[24,2,35]{2,1,0:T(2,128)(2,1)}, u32[]{:S(2)}) copy-start(bf16[24,2,35]{2,1,0:T(2,128)(2,1)} %param.9) | copy-start | bytes 10084
  33.8 5.9 %copy-start = (f32[256,384]{1,0:T(8,128)S(1)}, f32[256,384]{1,0:T(8,128)}, u32[]{:S(2)}) copy-start(f32[256,384]{1,0:T(8,128)} %param.8) | copy-start | bytes 1179652
  33.8 15.0 %all-to-all-start.1 = ((bf16[32,48,128]{2,1,0:T(8,128)(2,1)}), bf16[32,48,128]{2,1,0:T(8,128)(2,1)S(1)}, u32[]{:S(2)}, u32[]{:S(2)}) async-start(bf16[32,48,128]{2,1,0:T(8,128)(2,1)} %bitcast.6), calls=%async_computation.1 | async-start | bytes 786432 | tf_op jit(solution)/shard_map/all_to_all | solution.py:301

commit v6 on v5

--- a/solution.py
+++ b/solution.py
@@ -14,7 +14,9 @@
 TILE_R, TILE_C = 256, 384
 COL_R = TILE_R + 72
 FIELD_R = 304
-SPLIT = 144
+STEP = 80
+STEPS = 4
+COL_ROWS = (STEPS - 1) * STEP + BLK
 CHAN = 24
 SLOTS = 8
 PER_COL = 12 * ROWS
@@ -59,11 +61,16 @@
     return jnp.broadcast_to(slots[:, s : s + 1], (slots.shape[0], BLK))
 
 
-def pack_kernel(blocks_hbm, cells_hbm, out_hbm, blocks_ref, cells, stage, packed, ids_sem, in_sem, out_sem):
+def pack_kernel(
+    blocks_hbm, cells_hbm, owner_hbm, out_hbm, by_cell_ref, by_owner_ref,
+    blocks_ref, owner_ref, cells, stage, packed, ids_sem, owner_sem, in_sem, out_sem,
+):
     fetch_ids = pltpu.make_async_copy(blocks_hbm, blocks_ref, ids_sem)
     fetch_ids.start()
     fetch = pltpu.make_async_copy(cells_hbm, cells, in_sem)
     fetch.start()
+    fetch_owner = pltpu.make_async_copy(owner_hbm, owner_ref, owner_sem)
+    fetch_owner.start()
     lane = iota(1, (COLS, BLK))
     ids = jnp.full((COLS, BLK), -1.0, F32)
     for s in range(ROWS + 1, 8):
@@ -82,23 +89,21 @@
     ]
     for copy in copies:
         copy.start()
+    fetch_owner.wait()
+    by_cell_ref[...] = owner_select(owner_ref, False)
+    by_owner_ref[...] = owner_select(owner_ref, True)
     for copy in copies:
         copy.wait()
 
 
 def pick_kernel(
-    place_ref, first_ref, owner_hbm, out_ref, held_ref, slots_ref, by_owner_ref,
-    owner_ref, stage, mine, out_stage, sem,
+    place_ref, first_ref, by_cell_ref, out_ref, held_ref, slots_ref, stage, mine, out_stage,
 ):
-    fetch = pltpu.make_async_copy(owner_hbm, owner_ref, sem)
-    fetch.start()
     stage[...] = first_ref[...].astype(F32)
     slots = slot_ids(stage[pl.ds(ROWS, DEV, stride=8), :], place_ref[1])
     slots_ref[...] = slots
     table = jnp.concatenate([stage[pl.ds(s, DEV, stride=8), :] for s in range(ROWS)], 1)
-    fetch.wait()
-    by_owner_ref[...] = owner_select(owner_ref, True)
-    held = dot(owner_select(owner_ref, False), table.astype(BF)).astype(BF)
+    held = dot(by_cell_ref[...], table.astype(BF)).astype(BF)
     row = place_ref[0]
     own = held[:, :BLK].astype(F32)
     for s in range(1, ROWS):
@@ -120,13 +125,13 @@
     out_ref[...] = out_stage[...].astype(BF)
 
 
-def toeplitz(taps_ref, m, rows=BLK):
-    base = jnp.broadcast_to(taps_ref[pl.ds(m, 1), :], (rows, 2 * BLK))
+def toeplitz(taps_ref, m, rows=BLK, lanes=2 * BLK):
+    base = jnp.broadcast_to(taps_ref[pl.ds(m, 1), :lanes], (rows, lanes))
     return pltpu.roll(base, 0, 1, stride=1, stride_axis=0).astype(BF)
 
 
 def litho_kernel(
-    place_ref, weights_ref, recv_ref, target_ref, row_ref, row_flip_ref, col_ref, col_rev_ref,
+    place_ref, socs_ref, recv_ref, target_ref, row_ref, row_flip_ref, col_ref, col_rev_ref,
     out_ref, stage, wide, mask, columns_a, columns_b, field, light, grad, back_a, back_b,
 ):
     stage[...] = recv_ref[...].astype(F32)
@@ -139,7 +144,7 @@
     whole = jnp.concatenate([wide[q] for q in range(4)], 1)
     mask[...] = pltpu.roll(pltpu.roll(whole, HALF, 1), 2 * HALF, 0)[:COL_R].astype(BF)
     for columns in (columns_a, columns_b):
-        columns[:, COL_R:, :] = jnp.zeros((2, SPLIT + 2 * BLK - COL_R, TILE_C), BF)
+        columns[:, COL_R:, :] = jnp.zeros((2, COL_ROWS - COL_R, TILE_C), BF)
     light[...] = jnp.zeros_like(light)
 
     def make_columns(k, columns):
@@ -157,18 +162,21 @@
                 columns[r, :COL_R, q * BLK : (q + 1) * BLK] = made[:, r * BLK : (r + 1) * BLK]
 
     def make_field(k, columns):
-        row_matrix = jnp.concatenate([toeplitz(row_ref, 2 * k + r, FIELD_R - SPLIT) for r in range(2)], 1)
-        weight = weights_ref[k // 2]
+        row_matrix = jnp.concatenate([toeplitz(row_ref, 2 * k + r, STEP, BLK) for r in range(2)], 1)
+        weight = socs_ref[k // 2]
         windows = [
-            jnp.concatenate([columns[r, p * SPLIT : p * SPLIT + 2 * BLK, :] for r in range(2)], 0)
-            for p in range(2)
+            jnp.concatenate([columns[r, p * STEP : p * STEP + BLK, :] for r in range(2)], 0)
+            for p in range(STEPS)
         ]
-        last = dot(row_matrix, jnp.concatenate([w[:, 2 * BLK :] for w in windows], 1))
-        for p in range(2):
+        for p in range(STEPS):
+            if p % 2 == 0:
+                pair = jnp.concatenate([w[:, 2 * BLK :] for w in windows[p : p + 2]], 1)
+                last = dot(row_matrix, pair)
+            at = p % 2 * BLK
             made = jnp.concatenate(
-                [dot(row_matrix, windows[p][:, : 2 * BLK]), last[:, p * BLK : (p + 1) * BLK]], 1
+                [dot(row_matrix, windows[p][:, : 2 * BLK]), last[:, at : at + BLK]], 1
             )
-            here = slice(p * SPLIT, FIELD_R if p else SPLIT)
+            here = slice(p * STEP, min((p + 1) * STEP, FIELD_R))
             made = made[: here.stop - here.start]
             light[here] += weight * made * made
             field[k, here] = made
@@ -180,16 +188,20 @@
         if k + 1 < CHAN:
             make_columns(k + 1, buffers[(k + 1) % 2])
         make_field(k, buffers[k % 2])
-    resist = jax.nn.sigmoid(3.0 * (light[...] - 1.3))
+    total = socs_ref[0]
+    for n in range(1, CHAN // 2):
+        total += socs_ref[n]
+    total = jnp.full((1, TILE_C), total, F32)
+    resist = jax.nn.sigmoid(3.0 * (light[...] / total - 1.3))
     error = 2.0 * (resist - target_ref[...]) * 3.0 * resist * (1.0 - resist)
     at_row = iota(0, (FIELD_R, TILE_C))
     first = jnp.where(place_ref[0] == 0, HALF, 0)
     end = jnp.where(place_ref[0] == ROWS - 1, HALF + TILE_R, FIELD_R)
-    light[...] = jnp.where((at_row >= first) & (at_row < end), error, 0.0)
+    light[...] = jnp.where((at_row >= first) & (at_row < end), error * (2.0 / total), 0.0)
     grad[...] = jnp.zeros_like(grad)
 
     def make_back(k, j, back):
-        weighted = (2.0 * weights_ref[k // 2] * field[k] * light[...]).astype(BF)
+        weighted = (socs_ref[k // 2] * field[k] * light[...]).astype(BF)
         taps = jnp.concatenate([toeplitz(row_flip_ref, 2 * k + r) for r in range(2)], 0)
         windows = [
             weighted[: 2 * BLK],
@@ -282,12 +294,12 @@
 HBM = pl.BlockSpec(memory_space=pltpu.HBM)
 
 
-def call(kernel, out_shape, in_specs, scratch, limit=8, out_space=VMEM):
+def call(kernel, out_shape, in_specs, scratch, limit=8, out_space=None):
     return pl.pallas_call(
         kernel,
         out_shape=out_shape,
         in_specs=in_specs,
-        out_specs=jax.tree.map(lambda _: out_space, out_shape),
+        out_specs=out_space or jax.tree.map(lambda _: VMEM, out_shape),
         scratch_shapes=scratch,
         compiler_params=pltpu.CompilerParams(vmem_limit_bytes=limit << 20),
     )
@@ -304,7 +316,6 @@
 def per_device(cells, target, row_taps, col_taps, socs, cell_of_block, owner_map):
     struct = jax.ShapeDtypeStruct
     place = jnp.stack([lax.axis_index("row"), lax.axis_index("col")]).astype(jnp.int32)
-    weights = socs / jnp.sum(socs)
     owner = owner_map.reshape(1, DEV)
 
     def spread(taps, reverse):
@@ -328,36 +339,37 @@
         0,
     )
 
-    first = call(
+    select = struct((DEV, DEV), BF)
+    first, by_cell, by_owner = call(
         pack_kernel,
-        struct((DEV * 8, BLK), BF),
-        [HBM, HBM],
+        (struct((DEV * 8, BLK), BF), select, select),
+        [HBM, HBM, HBM],
         [
             pltpu.SMEM((2, 3), jnp.int32),
+            pltpu.VMEM((1, DEV), jnp.int32),
             pltpu.VMEM((BLK, BLK), F32),
             pltpu.VMEM((COLS * 8, BLK), F32),
             pltpu.VMEM((COLS * 8, BLK), BF),
             pltpu.SemaphoreType.DMA,
             pltpu.SemaphoreType.DMA,
+            pltpu.SemaphoreType.DMA,
             pltpu.SemaphoreType.DMA((ROWS,)),
         ],
-        out_space=HBM,
-    )(in_hbm(cell_of_block), in_hbm(cells.reshape(BLK, BLK)))
+        out_space=(HBM, VMEM, VMEM),
+    )(in_hbm(cell_of_block), in_hbm(cells.reshape(BLK, BLK)), in_hbm(owner))
     first = exchange(first.reshape(DEV, 8, BLK))
     first = first.reshape(DEV * 8, BLK)
 
-    picked, held, slots, by_owner = call(
+    picked, held, slots = call(
         pick_kernel,
-        (struct((COLS * PER_COL, BLK), BF), struct((BLK, BLK), F32), struct((DEV, BLK), F32), struct((DEV, DEV), BF)),
-        [SMEM, VMEM, HBM],
+        (struct((COLS * PER_COL, BLK), BF), struct((BLK, BLK), F32), struct((DEV, BLK), F32)),
+        [SMEM, VMEM, VMEM],
         [
-            pltpu.VMEM((1, DEV), jnp.int32),
             pltpu.VMEM((DEV * 8, BLK), F32),
             pltpu.VMEM((COLS, BLK), F32),
             pltpu.VMEM((COLS * PER_COL, BLK), F32),
-            pltpu.SemaphoreType.DMA,
         ],
-    )(place, first, in_hbm(owner))
+    )(place, first, by_cell)
     received = exchange(picked.reshape(COLS, PER_COL, BLK), "col")
     received = received.reshape(COLS * PER_COL, BLK)
 
@@ -369,8 +381,8 @@
             pltpu.VMEM((COLS * PER_COL, BLK), F32),
             pltpu.VMEM((4, 384, BLK), F32),
             pltpu.VMEM((COL_R, 512), BF),
-            pltpu.VMEM((2, SPLIT + 2 * BLK, TILE_C), BF),
-            pltpu.VMEM((2, SPLIT + 2 * BLK, TILE_C), BF),
+            pltpu.VMEM((2, COL_ROWS, TILE_C), BF),
+            pltpu.VMEM((2, COL_ROWS, TILE_C), BF),
             pltpu.VMEM((CHAN, FIELD_R, TILE_C), F32),
             pltpu.VMEM((FIELD_R, TILE_C), F32),
             pltpu.VMEM((TILE_R, 512), F32),
@@ -379,7 +391,7 @@
         ],
         32,
     )(
-        place, weights, received, wide_target,
+        place, in_hbm(socs), received, wide_target,
         spread(row_taps, False), spread(row_taps[:, :, ::-1], False),
         spread(col_taps, False), spread(col_taps, True),
     )

time: 94.8 us -> 87 us (0.918)
  waiting for transfers between devices: 17.5 us -> 15 us
  starting transfers between devices: 22.3 us -> 20.7 us
  local copies, waits for them, and re-layouts: 2.45 us -> 1.07 us
  Pallas kernels: 19.9 us -> 18.6 us
  other arithmetic: 1.52 us -> 0.27 us
    all_to_all x2, waiting for transfers between devices: 17.5 us -> 14.9 us  [exchange(): return lax.all_to_all(x, axes, 0, 0, tiled=True)]
  transfers between devices with their start and end apart: 4 -> 4, of which waited for: 2 -> 2; matrix products, arithmetic and copies ran while one was open for 2% -> 1% of each run, Pallas kernels for 4% -> 2%
where the time goes in v6:
time: 87 us; the launch traced here: 86.6 us
  blocking collectives  30.2 us (35%)
  starting transfers between devices  20.7 us (24%)
  Pallas kernels  18.6 us (21%)
  waiting for transfers between devices  15 us (17%)
  local copies, waits for them, and re-layouts  1.07 us (1%)
    all_to_all x2, blocking collectives, exchange(): return lax.all_to_all(x, axes, 0, 0, tiled=True)  30.2 us
    all_to_all x2, starting transfers between devices, exchange(): return lax.all_to_all(x, axes, 0, 0, tiled=True)  16.2 us
    all_to_all x2, waiting for transfers between devices, exchange(): return lax.all_to_all(x, axes, 0, 0, tiled=True)  14.9 us
    pallas_call x1, Pallas kernels, per_device(): call(litho_kernel, struct((DEV * SLOTS, BLK), BF), [SMEM] * 2 + [VMEM] *...  13.4 us
    ppermute x1, starting transfers between devices, per_device(): above = lax.ppermute(target[TILE_R - HALF:], 'row', down)  3.26 us
    pallas_call x1, Pallas kernels, per_device(): call(pick_kernel, (struct((COLS * PER_COL, BLK), BF), struct((BLK, BLK),...  2.06 us
  transfers between devices with their start and end apart: 4, of which 2 were waited for; matrix products, arithmetic and copies ran while one was open for 1% of the time, Pallas kernels for 2%

profile of v6, /device:TPU:1, one launch (start us, length us, event | category | flops | bytes accessed | tf_op | source)
XLA Modules:
  0.0 86.6 jit_solution(12115293771774750001)
XLA Ops:
  0.6 0.0 copy-start
  0.6 1.7 %shard_map.86 = (bf16[1024,128]{1,0:T(8,128)(2,1)}, bf16[128,128]{1,0:T(8,128)(2,1)S(1)}, bf16[128,128]{1,0:T(8,128)(2,1)S(1)}) custom-call(s32[2,3]{1,0:T(2,128)} %blocks_hbm.1, f32[128,128]{1,0:T(8,128)} %bitcast.26, s32[1,128]{1,0:T(1,128)} %bitcast.29), custom_call_target="tpu_custom_call" | custom-call | tf_op jit(solution)/shard_map/pallas_call | solution.py:343
  2.3 11.5 %all-to-all-start = ((bf16[128,8,128]{2,1,0:T(8,128)(2,1)}), bf16[128,8,128]{2,1,0:T(8,128)(2,1)S(1)}, u32[]{:S(2)}, u32[]{:S(2)}) async-start(bf16[128,8,128]{2,1,0:T(8,128)(2,1)} %bitcast.4), calls=%async_computation | async-start | bytes 524288 | tf_op jit(solution)/shard_map/all_to_all | solution.py:313
  13.8 0.0 copy-done
  13.8 0.0 copy-start.1
  13.9 3.3 %collective-permute-start = (f32[17,384]{1,0:T(8,128)S(1)}, f32[17,384]{1,0:T(8,128)S(1)}, u32[]{:S(2)}, u32[]{:S(2)}) collective-permute-start(f32[17,384]{1,0:T(8,128)S(1)} %get-tuple-element.18), channel_id=1, source_target_pairs={{0,32},{32,64},{64,96},{1,33},{33,65},{65,97},{2,34},{34,66},{66,9... | collective-permute-start | bytes 78344 | tf_op jit(solution)/shard_map/ppermute | solution.py:330
  17.1 1.3 %collective-permute-start.1 = (f32[17,384]{1,0:T(8,128)S(1)}, f32[17,384]{1,0:T(8,128)S(1)}, u32[]{:S(2)}, u32[]{:S(2)}) collective-permute-start(f32[17,384]{1,0:T(8,128)S(1)} %get-tuple-element.19), channel_id=1, source_target_pairs={{32,0},{64,32},{96,64},{33,1},{65,33},{97,65},{34,2},{66,34},{98,6... | collective-permute-start | bytes 78344 | tf_op jit(solution)/shard_map/ppermute | solution.py:331
  18.4 0.0 copy-done.1
  18.4 0.1 slice.17
  18.5 0.1 rev.7
  18.6 0.1 pad.6.clone
  18.7 0.1 pad_add_fusion.place_ref
  18.7 5.9 %all-to-all-done = bf16[128,8,128]{2,1,0:T(8,128)(2,1)S(1)} async-done(((bf16[128,8,128]{2,1,0:T(8,128)(2,1)}), bf16[128,8,128]{2,1,0:T(8,128)(2,1)S(1)}, u32[]{:S(2)}, u32[]{:S(2)}) %all-to-all-start) | async-done | bytes 262176 | tf_op jit(solution)/shard_map/all_to_all | solution.py:313
  24.6 2.1 %shard_map.87 = (bf16[1536,128]{1,0:T(8,128)(2,1)}, f32[128,128]{1,0:T(8,128)S(1)}, f32[128,128]{1,0:T(8,128)S(1)}) custom-call(s32[2]{0:T(128)S(1)} %pad_add_fusion.place_ref, bf16[1024,128]{1,0:T(8,128)(2,1)S(1)} %bitcast.18, bf16[128,128]{1,0:T(8,128)(2,1)S(1)} %get-tuple-element.11.by_cell_ref), custom_call_target="tpu_custom_call" | custom-call | tf_op jit(solution)/shard_map/pallas_call | solution.py:363
  26.7 4.7 %all-to-all-start.1 = ((bf16[32,48,128]{2,1,0:T(8,128)(2,1)}), bf16[32,48,128]{2,1,0:T(8,128)(2,1)S(1)}, u32[]{:S(2)}, u32[]{:S(2)}) async-start(bf16[32,48,128]{2,1,0:T(8,128)(2,1)} %bitcast.6), calls=%async_computation.1 | async-start | bytes 786432 | tf_op jit(solution)/shard_map/all_to_all | solution.py:313
  31.4 0.0 copy-start.2
  31.4 0.1 pad_maximum_fusion.col_rev_ref
  31.5 0.6 copy-done.2
  32.1 0.1 rev.6
  32.2 0.1 pad.11.clone
  32.3 0.0 collective-permute-done
  32.3 0.0 collective-permute-done.1
  32.3 0.1 maximum_maximum_fusion.target_ref
  32.4 9.1 %all-to-all-done.1 = bf16[32,48,128]{2,1,0:T(8,128)(2,1)S(1)} async-done(((bf16[32,48,128]{2,1,0:T(8,128)(2,1)}), bf16[32,48,128]{2,1,0:T(8,128)(2,1)S(1)}, u32[]{:S(2)}, u32[]{:S(2)}) %all-to-all-start.1) | async-done | bytes 393248 | tf_op jit(solution)/shard_map/all_to_all | solution.py:313
  41.5 13.4 %shard_map.88 = bf16[1024,128]{1,0:T(8,128)(2,1)S(1)} custom-call(s32[2]{0:T(128)S(1)} %pad_add_fusion.place_ref, f32[12]{0:T(128)} %socs_ref.1, bf16[1536,128]{1,0:T(8,128)(2,1)S(1)} %bitcast.17, f32[304,384]{1,0:T(8,128)S(1)} %maximum_maximum_fusion.target_ref, f32[48,256]{1,0:T(8,128)S(1)} %get-tuple-element.21.row_ref, ...), custom_call_target="tpu_custom_call" | custom-call | tf_op jit(solution)/shard_map/pallas_call | solution.py:376
  54.9 14.9 %all_to_all.20 = bf16[128,8,128]{2,1,0:T(8,128)(2,1)S(1)} all-to-all(bf16[128,8,128]{2,1,0:T(8,128)(2,1)S(1)} %bitcast.22), channel_id=1, replica_groups=mesh['row'=4,'col'=32] {'row','col'}, dimensions={0} | all-to-all | bytes 524288 | tf_op jit(solution)/shard_map/all_to_all | solution.py:313
  69.8 0.6 shard_map.89
  70.4 15.3 %all_to_all.21 = bf16[128,8,128]{2,1,0:T(8,128)(2,1)S(1)} all-to-all(bf16[128,8,128]{2,1,0:T(8,128)(2,1)S(1)} %bitcast.20), channel_id=1, replica_groups=mesh['row'=4,'col'=32] {'row','col'}, dimensions={0} | all-to-all | bytes 524288 | tf_op jit(solution)/shard_map/all_to_all | solution.py:313
  85.7 0.9 %shard_map.90 = (f32[128,128]{1,0:T(8,128)}, f32[256,384]{1,0:T(8,128)}) custom-call(bf16[1024,128]{1,0:T(8,128)(2,1)S(1)} %bitcast.21), custom_call_target="tpu_custom_call" | custom-call | tf_op jit(solution)/shard_map/pallas_call | solution.py:408
  (6 shorter events, 0.0 us)
Async XLA Ops:
  0.6 13.2 %copy-start = (f32[256,384]{1,0:T(8,128)S(1)}, f32[256,384]{1,0:T(8,128)}, u32[]{:S(2)}) copy-start(f32[256,384]{1,0:T(8,128)} %param.8) | copy-start | bytes 1179652
  2.3 22.3 %all-to-all-start = ((bf16[128,8,128]{2,1,0:T(8,128)(2,1)}), bf16[128,8,128]{2,1,0:T(8,128)(2,1)S(1)}, u32[]{:S(2)}, u32[]{:S(2)}) async-start(bf16[128,8,128]{2,1,0:T(8,128)(2,1)} %bitcast.4), calls=%async_computation | async-start | bytes 524288 | tf_op jit(solution)/shard_map/all_to_all | solution.py:313
  13.8 4.6 %copy-start.1 = (bf16[24,2,35]{2,1,0:T(2,128)(2,1)S(1)}, bf16[24,2,35]{2,1,0:T(2,128)(2,1)}, u32[]{:S(2)}) copy-start(bf16[24,2,35]{2,1,0:T(2,128)(2,1)} %param.10) | copy-start | bytes 10084
  13.9 18.5 %collective-permute-start = (f32[17,384]{1,0:T(8,128)S(1)}, f32[17,384]{1,0:T(8,128)S(1)}, u32[]{:S(2)}, u32[]{:S(2)}) collective-permute-start(f32[17,384]{1,0:T(8,128)S(1)} %get-tuple-element.18), channel_id=1, source_target_pairs={{0,32},{32,64},{64,96},{1,33},{33,65},{65,97},{2,34},{34,66},{66,9... | collective-permute-start | bytes 78344 | tf_op jit(solution)/shard_map/ppermute | solution.py:330
  17.1 15.2 %collective-permute-start.1 = (f32[17,384]{1,0:T(8,128)S(1)}, f32[17,384]{1,0:T(8,128)S(1)}, u32[]{:S(2)}, u32[]{:S(2)}) collective-permute-start(f32[17,384]{1,0:T(8,128)S(1)} %get-tuple-element.19), channel_id=1, source_target_pairs={{32,0},{64,32},{96,64},{33,1},{65,33},{97,65},{34,2},{66,34},{98,6... | collective-permute-start | bytes 78344 | tf_op jit(solution)/shard_map/ppermute | solution.py:331
  26.7 14.8 %all-to-all-start.1 = ((bf16[32,48,128]{2,1,0:T(8,128)(2,1)}), bf16[32,48,128]{2,1,0:T(8,128)(2,1)S(1)}, u32[]{:S(2)}, u32[]{:S(2)}) async-start(bf16[32,48,128]{2,1,0:T(8,128)(2,1)} %bitcast.6), calls=%async_computation.1 | async-start | bytes 786432 | tf_op jit(solution)/shard_map/all_to_all | solution.py:313
  31.4 0.7 copy-start.2

commit v7 on v6

--- a/solution.py
+++ b/solution.py
@@ -97,7 +97,8 @@
 
 
 def pick_kernel(
-    place_ref, first_ref, by_cell_ref, out_ref, held_ref, slots_ref, stage, mine, out_stage,
+    place_ref, first_ref, by_cell_ref, out_hbm, held_ref, slots_ref,
+    stage, mine, out_stage, packed, sem,
 ):
     stage[...] = first_ref[...].astype(F32)
     slots = slot_ids(stage[pl.ds(ROWS, DEV, stride=8), :], place_ref[1])
@@ -122,7 +123,15 @@
             made = jnp.where(wide_lane >= BLK // 2, made, picked[at : at + COLS])
         for s in range(ROWS):
             out_stage[pl.ds(ROWS * t + s, COLS, stride=PER_COL), :] = made[:, s * BLK : (s + 1) * BLK]
-    out_ref[...] = out_stage[...].astype(BF)
+    part = COLS * PER_COL // ROWS
+    copies = []
+    for n in range(ROWS):
+        here = pl.ds(n * part, part)
+        packed[here, :] = out_stage[here, :].astype(BF)
+        copies.append(pltpu.make_async_copy(packed.at[here], out_hbm.at[here], sem.at[n]))
+        copies[n].start()
+    for copy in copies:
+        copy.wait()
 
 
 def toeplitz(taps_ref, m, rows=BLK, lanes=2 * BLK):
@@ -276,17 +285,23 @@
     out_ref[...] = out_stage[...].astype(BF)
 
 
-def unpack_kernel(recv_ref, grad_ref, mask_ref, stage, wide):
+def unpack_kernel(recv_ref, grad_hbm, mask_hbm, stage, wide, grad, sem):
     stage[...] = recv_ref[...].astype(F32)
     for r in range(ROWS):
-        for p in range(2):
-            for q in range(3):
+        grad[pl.ds(r, COLS, stride=ROWS), :] = stage[pl.ds(r * COLS * 8 + 6, COLS, stride=8), :]
+    copies = [pltpu.make_async_copy(grad, grad_hbm, sem.at[3])]
+    copies[0].start()
+    for q in range(3):
+        for r in range(ROWS):
+            for p in range(2):
                 wide[q, pl.ds(p * BLK + r, COLS, stride=ROWS), :] = stage[
                     pl.ds(r * COLS * 8 + 3 * p + q, COLS, stride=8), :
                 ]
-        grad_ref[pl.ds(r, COLS, stride=ROWS), :] = stage[pl.ds(r * COLS * 8 + 6, COLS, stride=8), :]
-    for q in range(3):
-        mask_ref[:, q * BLK : (q + 1) * BLK] = wide[q]
+        here = pl.ds(q * BLK, BLK)
+        copies.append(pltpu.make_async_copy(wide.at[q], mask_hbm.at[:, here], sem.at[q]))
+        copies[q + 1].start()
+    for copy in copies:
+        copy.wait()
 
 
 SMEM = pl.BlockSpec(memory_space=pltpu.SMEM)
@@ -368,7 +383,10 @@
             pltpu.VMEM((DEV * 8, BLK), F32),
             pltpu.VMEM((COLS, BLK), F32),
             pltpu.VMEM((COLS * PER_COL, BLK), F32),
+            pltpu.VMEM((COLS * PER_COL, BLK), BF),
+            pltpu.SemaphoreType.DMA((ROWS,)),
         ],
+        out_space=(HBM, VMEM, VMEM),
     )(place, first, by_cell)
     received = exchange(picked.reshape(COLS, PER_COL, BLK), "col")
     received = received.reshape(COLS * PER_COL, BLK)
@@ -409,7 +427,13 @@
         unpack_kernel,
         (struct((BLK, BLK), F32), struct((TILE_R, TILE_C), F32)),
         [VMEM],
-        [pltpu.VMEM((DEV * 8, BLK), F32), pltpu.VMEM((3, TILE_R, BLK), F32)],
+        [
+            pltpu.VMEM((DEV * 8, BLK), F32),
+            pltpu.VMEM((3, TILE_R, BLK), F32),
+            pltpu.VMEM((BLK, BLK), F32),
+            pltpu.SemaphoreType.DMA((4,)),
+        ],
+        out_space=(HBM, HBM),
     )(results)
     return gradient.reshape(1, BLK, BLK), new_mask
 

time: 87 us -> 87.2 us (level)
  no operation moved by 1% of the time
where the time goes in v7:
time: 87.2 us; the launch traced here: 86.8 us
  blocking collectives  30.2 us (35%)
  starting transfers between devices  20.7 us (24%)
  Pallas kernels  18.6 us (21%)
  waiting for transfers between devices  15 us (17%)
  local copies, waits for them, and re-layouts  1.07 us (1%)
  between operations  0.95 us (1%)
    all_to_all x2, blocking collectives, exchange(): return lax.all_to_all(x, axes, 0, 0, tiled=True)  30.2 us
    all_to_all x2, starting transfers between devices, exchange(): return lax.all_to_all(x, axes, 0, 0, tiled=True)  16.2 us
    all_to_all x2, waiting for transfers between devices, exchange(): return lax.all_to_all(x, axes, 0, 0, tiled=True)  14.9 us
    pallas_call x1, Pallas kernels, per_device(): call(litho_kernel, struct((DEV * SLOTS, BLK), BF), [SMEM] * 2 + [VMEM] *...  13.4 us
    ppermute x1, starting transfers between devices, per_device(): above = lax.ppermute(target[TILE_R - HALF:], 'row', down)  3.26 us
    pallas_call x1, Pallas kernels, per_device(): call(pick_kernel, (struct((COLS * PER_COL, BLK), BF), struct((BLK, BLK),...  2.08 us
  transfers between devices with their start and end apart: 4, of which 2 were waited for; matrix products, arithmetic and copies ran while one was open for 1% of the time, Pallas kernels for 2%

profile of v7, /device:TPU:1, one launch (start us, length us, event | category | flops | bytes accessed | tf_op | source)
XLA Modules:
  0.0 86.8 jit_solution(7038745402752521714)
XLA Ops:
  0.6 0.0 copy-start
  0.6 1.7 %shard_map.86 = (bf16[1024,128]{1,0:T(8,128)(2,1)}, bf16[128,128]{1,0:T(8,128)(2,1)S(1)}, bf16[128,128]{1,0:T(8,128)(2,1)S(1)}) custom-call(s32[2,3]{1,0:T(2,128)} %blocks_hbm.1, f32[128,128]{1,0:T(8,128)} %bitcast.26, s32[1,128]{1,0:T(1,128)} %bitcast.29), custom_call_target="tpu_custom_call" | custom-call | tf_op jit(solution)/shard_map/pallas_call | solution.py:358
  2.3 11.5 %all-to-all-start = ((bf16[128,8,128]{2,1,0:T(8,128)(2,1)}), bf16[128,8,128]{2,1,0:T(8,128)(2,1)S(1)}, u32[]{:S(2)}, u32[]{:S(2)}) async-start(bf16[128,8,128]{2,1,0:T(8,128)(2,1)} %bitcast.4), calls=%async_computation | async-start | bytes 524288 | tf_op jit(solution)/shard_map/all_to_all | solution.py:328
  13.8 0.0 copy-done
  13.8 0.0 copy-start.1
  13.9 3.3 %collective-permute-start = (f32[17,384]{1,0:T(8,128)S(1)}, f32[17,384]{1,0:T(8,128)S(1)}, u32[]{:S(2)}, u32[]{:S(2)}) collective-permute-start(f32[17,384]{1,0:T(8,128)S(1)} %get-tuple-element.18), channel_id=1, source_target_pairs={{0,32},{32,64},{64,96},{1,33},{33,65},{65,97},{2,34},{34,66},{66,9... | collective-permute-start | bytes 78344 | tf_op jit(solution)/shard_map/ppermute | solution.py:345
  17.1 1.3 %collective-permute-start.1 = (f32[17,384]{1,0:T(8,128)S(1)}, f32[17,384]{1,0:T(8,128)S(1)}, u32[]{:S(2)}, u32[]{:S(2)}) collective-permute-start(f32[17,384]{1,0:T(8,128)S(1)} %get-tuple-element.19), channel_id=1, source_target_pairs={{32,0},{64,32},{96,64},{33,1},{65,33},{97,65},{34,2},{66,34},{98,6... | collective-permute-start | bytes 78344 | tf_op jit(solution)/shard_map/ppermute | solution.py:346
  18.4 0.0 copy-done.1
  18.4 0.1 slice.17
  18.5 0.1 rev.7
  18.6 0.1 pad.6.clone
  18.7 0.1 pad_add_fusion.place_ref
  18.7 5.9 %all-to-all-done = bf16[128,8,128]{2,1,0:T(8,128)(2,1)S(1)} async-done(((bf16[128,8,128]{2,1,0:T(8,128)(2,1)}), bf16[128,8,128]{2,1,0:T(8,128)(2,1)S(1)}, u32[]{:S(2)}, u32[]{:S(2)}) %all-to-all-start) | async-done | bytes 262176 | tf_op jit(solution)/shard_map/all_to_all | solution.py:328
  24.6 2.1 %shard_map.87 = (bf16[1536,128]{1,0:T(8,128)(2,1)}, f32[128,128]{1,0:T(8,128)S(1)}, f32[128,128]{1,0:T(8,128)S(1)}) custom-call(s32[2]{0:T(128)S(1)} %pad_add_fusion.place_ref, bf16[1024,128]{1,0:T(8,128)(2,1)S(1)} %bitcast.18, bf16[128,128]{1,0:T(8,128)(2,1)S(1)} %get-tuple-element.11.by_cell_ref), custom_call_target="tpu_custom_call" | custom-call | tf_op jit(solution)/shard_map/pallas_call | solution.py:378
  26.7 4.7 %all-to-all-start.1 = ((bf16[32,48,128]{2,1,0:T(8,128)(2,1)}), bf16[32,48,128]{2,1,0:T(8,128)(2,1)S(1)}, u32[]{:S(2)}, u32[]{:S(2)}) async-start(bf16[32,48,128]{2,1,0:T(8,128)(2,1)} %bitcast.6), calls=%async_computation.1 | async-start | bytes 786432 | tf_op jit(solution)/shard_map/all_to_all | solution.py:328
  31.4 0.0 copy-start.2
  31.4 0.1 pad_maximum_fusion.col_rev_ref
  31.5 0.6 copy-done.2
  32.1 0.1 rev.6
  32.3 0.1 pad.11.clone
  32.3 0.0 collective-permute-done
  32.4 0.0 collective-permute-done.1
  32.4 0.1 maximum_maximum_fusion.target_ref
  32.5 9.1 %all-to-all-done.1 = bf16[32,48,128]{2,1,0:T(8,128)(2,1)S(1)} async-done(((bf16[32,48,128]{2,1,0:T(8,128)(2,1)}), bf16[32,48,128]{2,1,0:T(8,128)(2,1)S(1)}, u32[]{:S(2)}, u32[]{:S(2)}) %all-to-all-start.1) | async-done | bytes 393248 | tf_op jit(solution)/shard_map/all_to_all | solution.py:328
  41.5 13.4 %shard_map.88 = bf16[1024,128]{1,0:T(8,128)(2,1)S(1)} custom-call(s32[2]{0:T(128)S(1)} %pad_add_fusion.place_ref, f32[12]{0:T(128)} %socs_ref.1, bf16[1536,128]{1,0:T(8,128)(2,1)S(1)} %bitcast.17, f32[304,384]{1,0:T(8,128)S(1)} %maximum_maximum_fusion.target_ref, f32[48,256]{1,0:T(8,128)S(1)} %get-tuple-element.21.row_ref, ...), custom_call_target="tpu_custom_call" | custom-call | tf_op jit(solution)/shard_map/pallas_call | solution.py:394
  54.9 14.9 %all_to_all.20 = bf16[128,8,128]{2,1,0:T(8,128)(2,1)S(1)} all-to-all(bf16[128,8,128]{2,1,0:T(8,128)(2,1)S(1)} %bitcast.22), channel_id=1, replica_groups=mesh['row'=4,'col'=32] {'row','col'}, dimensions={0} | all-to-all | bytes 524288 | tf_op jit(solution)/shard_map/all_to_all | solution.py:328
  69.9 0.6 shard_map.89
  70.4 15.3 %all_to_all.21 = bf16[128,8,128]{2,1,0:T(8,128)(2,1)S(1)} all-to-all(bf16[128,8,128]{2,1,0:T(8,128)(2,1)S(1)} %bitcast.20), channel_id=1, replica_groups=mesh['row'=4,'col'=32] {'row','col'}, dimensions={0} | all-to-all | bytes 524288 | tf_op jit(solution)/shard_map/all_to_all | solution.py:328
  85.8 0.8 shard_map.90
  (6 shorter events, 0.0 us)
Async XLA Ops:
  0.6 13.2 %copy-start = (f32[256,384]{1,0:T(8,128)S(1)}, f32[256,384]{1,0:T(8,128)}, u32[]{:S(2)}) copy-start(f32[256,384]{1,0:T(8,128)} %param.8) | copy-start | bytes 1179652
  2.3 22.3 %all-to-all-start = ((bf16[128,8,128]{2,1,0:T(8,128)(2,1)}), bf16[128,8,128]{2,1,0:T(8,128)(2,1)S(1)}, u32[]{:S(2)}, u32[]{:S(2)}) async-start(bf16[128,8,128]{2,1,0:T(8,128)(2,1)} %bitcast.4), calls=%async_computation | async-start | bytes 524288 | tf_op jit(solution)/shard_map/all_to_all | solution.py:328
  13.8 4.6 %copy-start.1 = (bf16[24,2,35]{2,1,0:T(2,128)(2,1)S(1)}, bf16[24,2,35]{2,1,0:T(2,128)(2,1)}, u32[]{:S(2)}) copy-start(bf16[24,2,35]{2,1,0:T(2,128)(2,1)} %param.10) | copy-start | bytes 10084
  13.9 18.5 %collective-permute-start = (f32[17,384]{1,0:T(8,128)S(1)}, f32[17,384]{1,0:T(8,128)S(1)}, u32[]{:S(2)}, u32[]{:S(2)}) collective-permute-start(f32[17,384]{1,0:T(8,128)S(1)} %get-tuple-element.18), channel_id=1, source_target_pairs={{0,32},{32,64},{64,96},{1,33},{33,65},{65,97},{2,34},{34,66},{66,9... | collective-permute-start | bytes 78344 | tf_op jit(solution)/shard_map/ppermute | solution.py:345
  17.1 15.2 %collective-permute-start.1 = (f32[17,384]{1,0:T(8,128)S(1)}, f32[17,384]{1,0:T(8,128)S(1)}, u32[]{:S(2)}, u32[]{:S(2)}) collective-permute-start(f32[17,384]{1,0:T(8,128)S(1)} %get-tuple-element.19), channel_id=1, source_target_pairs={{32,0},{64,32},{96,64},{33,1},{65,33},{97,65},{34,2},{66,34},{98,6... | collective-permute-start | bytes 78344 | tf_op jit(solution)/shard_map/ppermute | solution.py:346
  26.7 14.8 %all-to-all-start.1 = ((bf16[32,48,128]{2,1,0:T(8,128)(2,1)}), bf16[32,48,128]{2,1,0:T(8,128)(2,1)S(1)}, u32[]{:S(2)}, u32[]{:S(2)}) async-start(bf16[32,48,128]{2,1,0:T(8,128)(2,1)} %bitcast.6), calls=%async_computation.1 | async-start | bytes 786432 | tf_op jit(solution)/shard_map/all_to_all | solution.py:328
  31.4 0.7 copy-start.2
